TPU v7x, 768 devices: a whole 4x8x12 slice. The times are simulated.
768 devices in a mesh: sec: 3 (over z_hi), tp: 64 (over z_lo, y, core), blk: 4 (over x).
Axes of the slice: x: 4, y: 8, z: 12 (z_hi: 3, z_lo: 4; z = z_hi * 4 + z_lo), core: 2. Of those that a mesh axis runs over, the one named last changes fastest.
Arguments:
- perambulator: bfloat16 [64, 2, 2048, 2048], P('tp', None, 'blk'), may hold values from -0.125 to 0.125
- backward: bfloat16 [64, 2, 2048, 2048], P('tp', None, None, 'blk'), may hold values from -0.125 to 0.125
- elementals: bfloat16 [3, 64, 2, 2048, 128], P('sec', 'tp', None, 'blk'), may hold values from -6 to 6
- diagrams: int32 [64, 16, 2], P('tp'), may hold values from 0 to 63
- owner_loads: int32 [64], P('tp'), may hold values from 1 to 16, as said below
Outputs:
- hadron: float32 [3, 64, 2, 128, 128], P('sec', 'tp', None, 'blk')
Inputs may be any that keep to these rules, and one draw needn't show every extreme that they name: `diagrams`: pair indices of each owner's slots; slots at or past the owner's load are ignored. `owner_loads`: some owner has exactly 16 live slots.
All inputs are finite; a program needn't handle non-finite values.
Results may differ from a plain program's by a relative error of at most 0.007.
Values may be sent and summed in bfloat16 or wider, within the bound.
No kernel may reach another device: no remote copies, remote signals or barrier semaphores. Data moves between devices by JAX's collectives and lax.ppermute only.
A program may use at most 64 MiB of HBM per device.

v0:
```python
import jax
import jax.numpy as jnp
from jax import lax
from jax.sharding import Mesh
from jax.sharding import PartitionSpec as P

TP = ("tp_0", "tp_1", "tp_2")


def sent_to_all(shard, axis):
    devices = lax.axis_size(axis)
    return lax.all_to_all(
        jnp.broadcast_to(shard[None], (devices, *shard.shape)), axis, 0, 0, tiled=True
    )


def laid_out(parts, dim):
    parts = jnp.moveaxis(parts, 0, dim)
    dims = parts.shape
    return parts.reshape(*dims[:dim], dims[dim] * dims[dim + 1], *dims[dim + 2 :])


def collect(shard, axis, dim):
    parts = sent_to_all(shard, axis)
    return laid_out(parts, dim)


def split_up(shard, dim, devices):
    before, after = (shard.shape[:dim], shard.shape[dim + 1 :])
    return jnp.moveaxis(shard.reshape(*before, devices, -1, *after), dim, 0)


def sent_and_summed(shard, axis, dim):
    parts = split_up(shard, dim, lax.axis_size(axis))
    arrived = lax.all_to_all(parts, axis, split_axis=0, concat_axis=0, tiled=True)
    return arrived.sum(axis=0)


def passed_along(block, axis, distance):
    devices = range(lax.axis_size(axis))
    route = [((i - distance) % len(devices), i) for i in devices]
    return lax.ppermute(block, axis, route)


def taken_together(shard, axis):
    everything = sent_to_all(shard, axis)
    return jnp.sum(everything, axis=0)


def gather_in_order(shard, axes, sequence):
    parts = shard[None]
    for k in sequence:
        parts = lax.all_gather(parts, axes[k], axis=0, tiled=True)
    carried = [lax.axis_size(axes[k]) for k in reversed(sequence)]
    parts = parts.reshape(*carried, *shard.shape)
    turned = sorted(range(len(sequence)), key=lambda place: sequence[len(sequence) - 1 - place])
    return parts.transpose(*turned, *range(len(sequence), parts.ndim)).reshape(-1, *shard.shape)


def gather_axes(shard, axes, sequence, dim):
    return laid_out(gather_in_order(shard, axes, sequence), dim)


def complex_einsum(form, left_real, left_imag, right_real, right_imag, conj_left):
    if conj_left:
        real_part = jnp.einsum(
            form, left_real, right_real, preferred_element_type=jnp.float32
        ) + jnp.einsum(form, left_imag, right_imag, preferred_element_type=jnp.float32)
        imag_part = jnp.einsum(
            form, left_real, right_imag, preferred_element_type=jnp.float32
        ) - jnp.einsum(form, left_imag, right_real, preferred_element_type=jnp.float32)
    else:
        real_part = jnp.einsum(
            form, left_real, right_real, preferred_element_type=jnp.float32
        ) - jnp.einsum(form, left_imag, right_imag, preferred_element_type=jnp.float32)
        imag_part = jnp.einsum(
            form, left_real, right_imag, preferred_element_type=jnp.float32
        ) + jnp.einsum(form, left_imag, right_real, preferred_element_type=jnp.float32)
    return (real_part, imag_part)


def on_device(perambulator, backward, elementals, diagrams, owner_loads):
    tile_width = elementals.shape[4]
    full_order = perambulator.shape[3]
    source = elementals[0]
    tile_piece = collect(elementals, "blk", 3)[0]
    real_part, imag_part = complex_einsum(
        "prc,pck->prk",
        perambulator[:, 0],
        perambulator[:, 1],
        tile_piece[:, 0],
        tile_piece[:, 1],
        False,
    )
    first_image = jnp.stack([real_part, imag_part], axis=1).astype(jnp.bfloat16)
    real_part, imag_part = complex_einsum(
        "pri,pik->rpk", backward[:, 0], backward[:, 1], first_image[:, 0], first_image[:, 1], False
    )
    dressed_elementals = sent_and_summed(
        jnp.stack([real_part, imag_part], axis=2), "blk", 0
    ).astype(jnp.bfloat16)
    sink_block_tiles = passed_along(source, "sec", 1)
    norm_scale = full_order ** (-0.5)
    block_real, block_imag = complex_einsum(
        "ild,lio->ido",
        sink_block_tiles[:, 0],
        sink_block_tiles[:, 1],
        dressed_elementals[:, :, 0],
        dressed_elementals[:, :, 1],
        True,
    )
    partial_value = jnp.stack([block_real, block_imag], axis=1) * norm_scale
    owner_list = diagrams[0]
    owner_load = owner_loads[0]
    slot_count = owner_list.shape[0]
    quarter = tile_width // lax.axis_size("blk")
    share_index = lax.axis_index("blk")
    blocks = taken_together(partial_value, "blk").astype(jnp.bfloat16)
    received_pieces = gather_axes(blocks, TP, (0, 1, 2), 0)
    piece_ids = jnp.arange(received_pieces.shape[0], dtype=jnp.int32)
    left_select = (owner_list[:, 0:1] == piece_ids[None, :]).astype(jnp.bfloat16)
    right_select = (owner_list[:, 1:2] == piece_ids[None, :]).astype(jnp.bfloat16)
    left_select, right_select = (left_select, right_select)
    share_rows = lax.dynamic_slice_in_dim(received_pieces, share_index * quarter, quarter, 2)
    left_addition = jnp.einsum(
        "gj,jcrk->gcrk", left_select, share_rows, preferred_element_type=jnp.float32
    )
    right_add = jnp.einsum(
        "gj,jcrk->gcrk", right_select, received_pieces, preferred_element_type=jnp.float32
    )
    left_blocks = left_addition
    right_blocks = right_add
    left_blocks = left_blocks.astype(jnp.bfloat16)
    right_blocks = right_blocks.astype(jnp.bfloat16)
    active = (jnp.arange(slot_count, dtype=jnp.int32) < owner_load).astype(jnp.bfloat16)
    masked = left_blocks * active[:, None, None, None]
    left_flat = jnp.transpose(masked, (1, 2, 0, 3)).reshape(2, quarter, slot_count * tile_width)
    right_flat = jnp.transpose(right_blocks, (1, 0, 2, 3)).reshape(
        2, slot_count * tile_width, tile_width
    )
    hadron_real, hadron_imag = complex_einsum(
        "rk,km->rm", left_flat[0], left_flat[1], right_flat[0], right_flat[1], False
    )
    total = jnp.stack([hadron_real, hadron_imag], axis=0)
    total = total * (tile_width * slot_count) ** (-0.5)
    return total.reshape(1, 1, 2, quarter, tile_width)


def solution(mesh):
    torus = Mesh(
        mesh.devices.reshape(mesh.shape["sec"], 4, 8, 2, mesh.shape["blk"]),
        ("sec", "tp_0", "tp_1", "tp_2", "blk"),
    )
    in_specs = (
        P(TP, None, "blk", None),
        P(TP, None, None, "blk"),
        P("sec", TP, None, "blk", None),
        P(TP, None, None),
        P(TP),
    )
    out_specs = P("sec", TP, None, "blk", None)
    return jax.shard_map(
        on_device, mesh=torus, in_specs=in_specs, out_specs=out_specs, check_vma=False
    )
```

profile of v0, /device:TPU:1, one launch (start us, length us, event | category | flops | bytes accessed | tf_op | source)
XLA Modules:
  0.0 201.2 jit_solution(9949242011129839789)
XLA Ops:
  6.5 0.0 copy-start.4
  6.5 1.2 broadcast_in_dim.7
  7.8 14.5 %all_to_all.15 = bf16[4,1,1,2,512,128]{5,4,3,2,1,0:T(8,128)(2,1)S(1)} all-to-all(bf16[4,1,1,2,512,128]{5,4,3,2,1,0:T(8,128)(2,1)S(1)} %broadcast_in_dim.7), channel_id=1, replica_groups=mesh['sec'=3,'tp_0'=4,'tp_1'=8,'tp_2'=2,'blk'=4] {'blk'}, dimensions={0} | all-to-all | bytes 2097152 | tf_op jit(solution)/shard_map/all_to_all | solution.py:12
  22.3 0.1 copy.38
  22.4 0.0 copy-done.4
  22.4 0.7 fusion.10
  23.1 0.7 fusion.8
  23.8 0.0 copy-start.1
  23.8 0.7 fusion.36
  24.5 0.7 fusion.33
  25.3 0.7 copy-done.1
  26.0 0.8 fusion.6
  26.8 0.8 fusion.4
  27.7 0.8 fusion.1
  28.5 0.7 stack.30
  29.2 0.3 copy.39
  29.6 2.4 %fusion = f32[2048,1,128]{0,2,1:T(8,128)S(1)} fusion(f32[128,2048]{1,0:T(8,128)S(1)} %fusion.4, bf16[512,128]{1,0:T(8,128)(2,1)S(1)} %fusion.36, bf16[1,2,2048,512]{3,2,1,0:T(8,128)(2,1)} %param.6), kind=kOutput, calls=%fused_computation.1 | convolution fusion | flops 268697600 | bytes 4325376 | tf_op jit(solution)/shard_map/pri,pik->rpk/dot_general | solution.py:78
  32.0 0.7 stack.31
  32.7 0.3 copy.40
  33.1 0.0 copy-start.2
  33.1 1.6 pad_maximum_fusion
  34.7 3.6 %all-to-all-start.1 = ((f32[4,512,1,2,128]{1,4,3,2,0:T(8,128)}), f32[4,512,1,2,128]{1,4,3,2,0:T(8,128)S(1)}, u32[]{:S(2)}, u32[]{:S(2)}) async-start(f32[4,512,1,2,128]{1,4,3,2,0:T(8,128)} %pad_maximum_fusion), calls=%async_computation.1 | async-start | bytes 4194304 | tf_op jit(solution)/shard_map/all_to_all | solution.py:35
  38.3 0.0 all-gather.4.cloned.1.call-start
  38.4 0.0 copy-done.2
  38.4 0.0 copy-start.3
  38.4 15.1 %collective-permute-start = (bf16[1,2,512,128]{3,2,1,0:T(8,128)(2,1)S(1)}, bf16[1,2,512,128]{3,2,1,0:T(8,128)(2,1)S(1)}, u32[]{:S(2)}, u32[]{:S(2)}) collective-permute-start(bf16[1,2,512,128]{3,2,1,0:T(8,128)(2,1)S(1)} %bitcast.166), channel_id=1, source_target_pairs={{512,0},{0,256},{256,512},{513,1},{1,257},{257,513},{514,2},{2,258... | collective-permute-start | bytes 786440 | tf_op jit(solution)/shard_map/ppermute | solution.py:42
  53.5 1.5 all-to-all-done.1
  55.0 0.2 reduce_sum.18
  55.2 7.0 %collective-permute-done = bf16[1,2,512,128]{3,2,1,0:T(8,128)(2,1)S(1)} collective-permute-done((bf16[1,2,512,128]{3,2,1,0:T(8,128)(2,1)S(1)}, bf16[1,2,512,128]{3,2,1,0:T(8,128)(2,1)S(1)}, u32[]{:S(2)}, u32[]{:S(2)}) %collective-permute-start) | collective-permute-done | bytes 262176 | tf_op jit(solution)/shard_map/ppermute | solution.py:42
  62.2 0.2 fusion.47
  62.4 0.2 fusion.46
  62.5 0.2 fusion.40
  62.7 0.2 fusion.39
  62.9 0.1 copy.44
  63.1 10.6 %all_to_all.16 = f32[4,1,2,128,128]{4,3,2,1,0:T(8,128)S(1)} all-to-all(f32[4,1,2,128,128]{4,3,2,1,0:T(8,128)S(1)} %broadcast_in_dim.8), channel_id=1, replica_groups=mesh['sec'=3,'tp_0'=4,'tp_1'=8,'tp_2'=2,'blk'=4] {'blk'}, dimensions={0} | all-to-all | bytes 1048576 | tf_op jit(solution)/shard_map/all_to_all | solution.py:12
  73.7 31.9 %all-gather = bf16[8,128,128]{2,1,0:T(8,128)(2,1)} all-gather(bf16[2,128,128]{2,1,0:T(8,128)(2,1)S(1)} %reduce_sum.19), channel_id=2, replica_groups=mesh['sec'=3,'tp_0'=4,'tp_1'=8,'tp_2'=2,'blk'=4] {'tp_0'}, dimensions={0}, use_global_device_ids=true | all-gather | bytes 327680 | tf_op jit(solution)/shard_map/all_gather | solution.py:53
  105.6 0.0 all-gather.4.cloned.1.call-update
  105.6 0.2 all-gather.6.cloned.1.call-start
  105.8 41.9 %all-gather.4.cloned.1.call-done = bf16[32,1,2,128,128]{4,3,2,1,0:T(8,128)(2,1)} async-done(((bf16[4,1,2,128,128]{4,3,2,1,0:T(8,128)(2,1)}), bf16[32,1,2,128,128]{4,3,2,1,0:T(8,128)(2,1)}) %all-gather.4.cloned.1.call-update) | async-done | bytes 2097168 | tf_op jit(solution)/shard_map/all_gather | solution.py:53
  147.7 0.0 all-gather.6.cloned.1.call-update
  148.4 0.0 copy-done.3
  148.4 31.4 %all-gather.6.cloned.1.call-done = bf16[64,1,2,128,128]{4,3,2,1,0:T(8,128)(2,1)} async-done(((bf16[32,1,2,128,128]{4,3,2,1,0:T(8,128)(2,1)}), bf16[64,1,2,128,128]{4,3,2,1,0:T(8,128)(2,1)}) %all-gather.6.cloned.1.call-update) | async-done | bytes 4194320 | tf_op jit(solution)/shard_map/all_gather | solution.py:53
  179.8 6.5 %copy.46 = bf16[4,8,2,1,2,128,128]{6,2,1,0,5,4,3:T(2,128)(2,1)S(1)} copy(bf16[4,8,2,1,2,128,128]{6,5,4,0,1,2,3:T(8,128)(2,1)} %bitcast.155) | data formatting | bytes 8388608 | tf_op jit(solution)/shard_map/transpose | solution.py:57
  186.4 0.0 copy-start
  186.4 1.9 copy-done
  188.3 0.3 fusion.32
  188.6 0.5 copy.48
  189.1 2.9 %fusion.24 = bf16[2,16,128,128]{3,1,2,0:T(8,128)(2,1)S(1)} fusion(bf16[64,2,128,128]{3,0,2,1:T(8,128)(2,1)} %bitcast.154, s32[16]{0:T(128)S(1)} %get-tuple-element.7), kind=kOutput, calls=%fused_computation.28 | convolution fusion | flops 67634176 | bytes 5242944 | tf_op jit(solution)/shard_map/gj,jcrk->gcrk/dot_general | solution.py:128
  192.0 0.3 convolution_bitcast_fusion.2
  192.3 0.3 convolution_bitcast_fusion
  192.6 0.5 copy.47
  193.1 0.3 fusion.42
  193.4 0.3 fusion.44
  193.7 0.6 maximum_multiply_fusion.1
  (6 shorter events, 0.1 us)
Async XLA Ops:
  6.5 15.8 %copy-start.4 = (bf16[1,2,512,2048]{3,2,1,0:T(8,128)(2,1)S(1)}, bf16[1,2,512,2048]{3,2,1,0:T(8,128)(2,1)}, u32[]{:S(2)}) copy-start(bf16[1,2,512,2048]{3,2,1,0:T(8,128)(2,1)} %param.5) | copy-start | bytes 12582916
  23.8 2.2 %copy-start.1 = (bf16[1,2,2048,512]{3,2,1,0:T(8,128)(2,1)S(1)}, bf16[1,2,2048,512]{3,2,1,0:T(8,128)(2,1)}, u32[]{:S(2)}) copy-start(bf16[1,2,2048,512]{3,2,1,0:T(8,128)(2,1)} %param.6) | copy-start | bytes 12582916
  33.1 5.3 %copy-start.2 = (bf16[1,1,2,512,128]{4,3,2,1,0:T(8,128)(2,1)S(1)}, bf16[1,1,2,512,128]{4,3,2,1,0:T(8,128)(2,1)}, u32[]{:S(2)}) copy-start(bf16[1,1,2,512,128]{4,3,2,1,0:T(8,128)(2,1)} %param.7) | copy-start | bytes 786436
  34.7 20.3 %all-to-all-start.1 = ((f32[4,512,1,2,128]{1,4,3,2,0:T(8,128)}), f32[4,512,1,2,128]{1,4,3,2,0:T(8,128)S(1)}, u32[]{:S(2)}, u32[]{:S(2)}) async-start(f32[4,512,1,2,128]{1,4,3,2,0:T(8,128)} %pad_maximum_fusion), calls=%async_computation.1 | async-start | bytes 4194304 | tf_op jit(solution)/shard_map/all_to_all | solution.py:35
  38.3 109.4 %all-gather.4.cloned.1.call-start = ((), (), s32[]{:S(2)}) async-start(), calls=%async_computation.3 | async-start | bytes 2359296 | tf_op jit(solution)/shard_map/all_gather | solution.py:53
  38.4 110.1 %copy-start.3 = (s32[1,16,2]{1,2,0:T(2,128)S(1)}, s32[1,16,2]{1,2,0:T(2,128)}, u32[]{:S(2)}) copy-start(s32[1,16,2]{1,2,0:T(2,128)} %param.8) | copy-start | bytes 388
  38.4 23.8 %collective-permute-start = (bf16[1,2,512,128]{3,2,1,0:T(8,128)(2,1)S(1)}, bf16[1,2,512,128]{3,2,1,0:T(8,128)(2,1)S(1)}, u32[]{:S(2)}, u32[]{:S(2)}) collective-permute-start(bf16[1,2,512,128]{3,2,1,0:T(8,128)(2,1)S(1)} %bitcast.166), channel_id=1, source_target_pairs={{512,0},{0,256},{256,512},{513,1},{1,257},{257,513},{514,2},{2,258... | collective-permute-start | bytes 786440 | tf_op jit(solution)/shard_map/ppermute | solution.py:42
  105.6 74.2 %all-gather.6.cloned.1.call-start = ((), (), s32[]{:S(2)}) async-start(), calls=%async_computation.4 | async-start | bytes 6291456 | tf_op jit(solution)/shard_map/all_gather | solution.py:53
  186.4 1.9 copy-start
Sparse Core Ops, SparseCore 0:
  105.7 41.9 all-gather.3
  150.1 29.6 all-gather.5
where the time goes:
time: 202 us; the launch traced here: 201 us
  waiting for transfers between devices  81.7 us (40%)
  blocking collectives  57 us (28%)
  starting transfers between devices  19 us (9%)
  between operations  14.4 us (7%)
  local copies, waits for them, and re-layouts  13.7 us (7%)
  matrix products  12.8 us (6%)
  other arithmetic  2.53 us (1%)
    all_gather x2, waiting for transfers between devices, gather_in_order(): parts = lax.all_gather(parts, axes[k], axis=0, tiled=True)  73.2 us
    all_gather x1, blocking collectives, gather_in_order(): parts = lax.all_gather(parts, axes[k], axis=0, tiled=True)  31.9 us
    all_to_all x2, blocking collectives, sent_to_all(): lax.all_to_all(jnp.broadcast_to(shard[None], (devices, *shard.shape)), ax...  25.1 us
    ppermute x1, starting transfers between devices, passed_along(): return lax.ppermute(block, axis, route)  15.1 us
    ppermute x1, waiting for transfers between devices, passed_along(): return lax.ppermute(block, axis, route)  6.96 us
    transpose x1, local copies, waits for them, and re-layouts, gather_in_order(): parts.transpose(*turned, *range(len(sequence), parts.ndim))  6.54 us
  transfers between devices with their start and end apart: 4, of which 4 were waited for; matrix products, arithmetic and copies ran while one was open for 0% of the time, Pallas kernels for 0%

commit v1 on v0

v1 whole, which is shorter than its diff:
```python
import jax
import jax.numpy as jnp
from jax import lax
from jax.experimental import pallas as pl
from jax.experimental.pallas import tpu as pltpu
from jax.sharding import Mesh
from jax.sharding import PartitionSpec as P

TP = ("z", "y", "c")
BF16 = jnp.bfloat16
F32 = jnp.float32
VMEM = pl.BlockSpec(memory_space=pltpu.VMEM)
SMEM = pl.BlockSpec(memory_space=pltpu.SMEM)


def dot(a, b, ca, cb):
    return lax.dot_general(a, b, (((ca,), (cb,)), ((), ())), preferred_element_type=F32)


def image_kernel(tau_ref, tile_ref, image_ref):
    parts, _, rows, k = tile_ref.shape
    acc_r = acc_i = None
    for j in range(parts):
        both = jnp.concatenate([tile_ref[j, 0], tile_ref[j, 1]], axis=1)
        add_r = dot(tau_ref[0, :, j * rows : (j + 1) * rows], both, 1, 0)
        add_i = dot(tau_ref[1, :, j * rows : (j + 1) * rows], both, 1, 0)
        acc_r = add_r if acc_r is None else acc_r + add_r
        acc_i = add_i if acc_i is None else acc_i + add_i
    image_ref[0] = (acc_r[:, :k] - acc_i[:, k:]).astype(BF16)
    image_ref[1] = (acc_r[:, k:] + acc_i[:, :k]).astype(BF16)


def left_kernel(beta_ref, tile_ref, left_ref):
    parts, _, rows, k = tile_ref.shape
    acc_r = acc_i = None
    for j in range(parts):
        both = jnp.concatenate([tile_ref[j, 0], tile_ref[j, 1]], axis=1)
        add_r = dot(both, beta_ref[0, j * rows : (j + 1) * rows, :], 0, 0)
        add_i = dot(both, beta_ref[1, j * rows : (j + 1) * rows, :], 0, 0)
        acc_r = add_r if acc_r is None else acc_r + add_r
        acc_i = add_i if acc_i is None else acc_i + add_i
    left_ref[0] = (acc_r[:k] + acc_i[k:]).astype(BF16)
    left_ref[1] = (acc_i[:k] - acc_r[k:]).astype(BF16)


def pack_kernel(scale, left_ref, image_ref, meta_ref, out_ref):
    slices = out_ref.shape[0]
    k = image_ref.shape[2]
    both = jnp.concatenate([image_ref[0], image_ref[1]], axis=1)
    from_r = dot(left_ref[0], both, 1, 0)
    from_i = dot(left_ref[1], both, 1, 0)
    real = (from_r[:, :k] - from_i[:, k:]) * scale
    imag = (from_r[:, k:] + from_i[:, :k]) * scale
    cut = [
        x.reshape(slices, k // slices, k) for x in (real.T, imag.T, real, imag)
    ]
    packed = jnp.concatenate(cut, axis=1).astype(BF16)
    n = packed.shape[1]
    out_ref[:, :n, :] = packed
    out_ref[:, n:, :] = jnp.broadcast_to(meta_ref[...][None], (slices, *meta_ref.shape))


def sum_kernel(in_ref, out_ref):
    copies, pairs, rows, _ = out_ref.shape
    parts = in_ref.shape[0] // pairs
    for q in range(pairs):
        total = in_ref[q * parts, :rows, :].astype(F32)
        for j in range(1, parts):
            total = total + in_ref[q * parts + j, :rows, :].astype(F32)
        total = total.astype(BF16)
        for y in range(copies):
            out_ref[y, q] = total


def product_kernel(slots, ny, nc, meta_ref, own_ref, other_ref, out_ref):
    owners = out_ref.shape[0]
    quarters, _, rows, k = out_ref.shape[1:]
    w = own_ref.shape[2] // 4
    for o in range(owners):
        mine = meta_ref[o, 2 * slots + 1]
        load = meta_ref[o, 2 * slots]

        def fetch(p):
            z = p // (ny * nc)
            y = (p // nc) % ny
            here = own_ref[y, z]
            there = other_ref[y, z]
            return jnp.where((p % nc) == mine, here, there).astype(F32)

        lefts, reals, imags = [], [], []
        for g in range(slots):
            left = fetch(meta_ref[o, 2 * g])[: 2 * w]
            right = fetch(meta_ref[o, 2 * g + 1])[2 * w :]
            lefts.append(jnp.where(g < load, left, jnp.zeros_like(left)))
            reals += [right[:w], -right[w:]]
            imags += [right[w:], right[:w]]
        left = jnp.concatenate(lefts, axis=0).astype(BF16)
        right = jnp.concatenate(
            [jnp.concatenate(reals, axis=0), jnp.concatenate(imags, axis=0)], axis=1
        ).astype(BF16)
        both = dot(left, right, 0, 0)
        for q in range(quarters):
            for c in range(2):
                out_ref[o, q, c] = both[q * rows : (q + 1) * rows, c * k : (c + 1) * k].astype(BF16)


def call(kernel, out, specs, name, flops=0, moved=0):
    return pl.pallas_call(
        kernel,
        out_shape=jax.ShapeDtypeStruct(*out),
        in_specs=specs,
        out_specs=VMEM,
        name=name,
        cost_estimate=pl.CostEstimate(flops=flops, bytes_accessed=moved, transcendentals=0),
    )


def on_device(perambulator, backward, elementals, diagrams, owner_loads):
    tau, beta = perambulator[0], backward[0]
    tile = elementals[0, 0]
    _, share, k = tile.shape
    order = tau.shape[2]
    nx, nz, ny, nc = (lax.axis_size(a) for a in ("blk", "z", "y", "c"))
    ns = lax.axis_size("sec")
    slots = diagrams.shape[1]
    slices = nz * nx
    w = k // slices
    quarter = k // nx

    tiles = lax.all_to_all(
        jnp.broadcast_to(tile[None], (nx, *tile.shape)), "blk", 0, 0, tiled=True
    )
    left = call(left_kernel, ((2, k, share), BF16), [VMEM] * 2, "left", 8 * k * order * share, 2**22)(
        beta, tiles
    )
    left = lax.ppermute(left, "sec", [((i - 1) % ns, i) for i in range(ns)])
    image = call(image_kernel, ((2, share, k), BF16), [VMEM] * 2, "image", 8 * k * order * share, 2**22)(
        tau, tiles
    )

    lists = jnp.concatenate([diagrams[0].reshape(-1), owner_loads]).astype(BF16)
    meta = jnp.zeros((16, k), BF16).at[0, : 2 * slots + 1].set(lists)
    packed = call(
        lambda *refs: pack_kernel(order**-0.5, *refs),
        ((slices, 4 * w + 16, k), BF16),
        [VMEM] * 3,
        "pack",
    )(left, image, meta)
    packed = lax.all_to_all(packed, ("z", "blk"), 0, 0, tiled=True)
    pieces = call(sum_kernel, ((ny, nz, 4 * w, k), BF16), [VMEM], "sum")(packed)
    pieces = lax.all_to_all(pieces, "y", 0, 0, tiled=True)
    others = lax.ppermute(pieces, "c", [(i, (i + 1) % nc) for i in range(nc)])

    numbers = packed.reshape(nz, nx, 4 * w + 16, k)[:, 0, 4 * w, :].astype(jnp.int32)
    column = lax.broadcasted_iota(jnp.int32, numbers.shape, 1)
    numbers = jnp.where(column == 2 * slots + 1, lax.axis_index("c"), numbers)
    partial = call(
        lambda *refs: product_kernel(slots, ny, nc, *refs),
        ((nz, nx, 2, quarter, k), BF16),
        [SMEM, VMEM, VMEM],
        "product",
    )(numbers, pieces, others)
    arrived = lax.all_to_all(
        partial.reshape(slices, 2, quarter, k), ("z", "blk"), 0, 0, tiled=True
    )
    total = jnp.sum(arrived.astype(F32), axis=0) * (k * slots) ** (-0.5)
    return total.reshape(1, 1, 2, quarter, k)


def solution(mesh):
    torus = Mesh(
        mesh.devices.reshape(mesh.shape["sec"], 4, 8, 2, mesh.shape["blk"]),
        ("sec", "z", "y", "c", "blk"),
    )
    in_specs = (
        P(TP, None, "blk", None),
        P(TP, None, None, "blk"),
        P("sec", TP, None, "blk", None),
        P(TP, None, None),
        P(TP),
    )
    out_specs = P("sec", TP, None, "blk", None)
    return jax.shard_map(
        on_device, mesh=torus, in_specs=in_specs, out_specs=out_specs, check_vma=False
    )
```

time: 202 us -> 123 us (0.61)
  waiting for transfers between devices: 81.7 us -> 2.88 us
  blocking collectives: 57 us -> 77.3 us
  Pallas kernels: 0 us -> 16.1 us
  between operations: 14.4 us -> 0.72 us
  matrix products: 12.8 us -> 0 us
  local copies, waits for them, and re-layouts: 13.7 us -> 3.38 us
    all_gather x2 -> x0, waiting for transfers between devices: 73.2 us -> none  [gather_in_order(): parts = lax.all_gather(parts, axes[k], axis=0, tiled=True)]
    all_to_all x2 -> x4, blocking collectives: 25.1 us -> 77.3 us  [the longest x1 32.3 us: on_device(): packed = lax.all_to_all(packed, ('z', 'blk'), 0, 0, tiled=True)]
    all_gather x1 -> x0, blocking collectives: 31.9 us -> none  [gather_in_order(): parts = lax.all_gather(parts, axes[k], axis=0, tiled=True)]
    pallas_call x0 -> x5, Pallas kernels: none -> 16.1 us  [the longest x1 4.46 us: on_device(): call(image_kernel, ((2, share, k), BF16), [VMEM] * 2, 'image', 8 * k * or...]
    dot_general x18 -> x0, matrix products: 12.8 us -> none  [the longest x4 3.59 us: complex_einsum(): jnp.einsum(form, left_imag, right_real, preferred_element_type=jnp.float32)]
    transpose x1 -> x0, local copies, waits for them, and re-layouts: 6.54 us -> none  [gather_in_order(): parts.transpose(*turned, *range(len(sequence), parts.ndim))]
    ppermute x1 -> x2, starting transfers between devices: 15.1 us -> 20.4 us  [the longest x1 15.1 us: on_device(): left = lax.ppermute(left, 'sec', [((i - 1) % ns, i) for i in range(ns)])]
    ppermute x1 -> x2, waiting for transfers between devices: 6.96 us -> 2.88 us  [the longest x1 2.88 us: on_device(): left = lax.ppermute(left, 'sec', [((i - 1) % ns, i) for i in range(ns)])]
  transfers between devices with their start and end apart: 4 -> 2, of which waited for: 4 -> 1; matrix products, arithmetic and copies ran while one was open for 0% -> 2% of each run, Pallas kernels for 0% -> 4%
where the time goes in v1:
time: 123 us
  blocking collectives  77.3 us (63%)
  starting transfers between devices  20.4 us (17%)
  Pallas kernels  16.1 us (13%)
  local copies, waits for them, and re-layouts  3.38 us (3%)
  waiting for transfers between devices  2.88 us (2%)
  other arithmetic  1.93 us (2%)
    all_to_all x1, blocking collectives, on_device(): packed = lax.all_to_all(packed, ('z', 'blk'), 0, 0, tiled=True)  32.3 us
    all_to_all x1, blocking collectives, on_device(): pieces = lax.all_to_all(pieces, 'y', 0, 0, tiled=True)  16.2 us
    ppermute x1, starting transfers between devices, on_device(): left = lax.ppermute(left, 'sec', [((i - 1) % ns, i) for i in range(ns)])  15.1 us
    all_to_all x1, blocking collectives, on_device(): lax.all_to_all(jnp.broadcast_to(tile[None], (nx, *tile.shape)), 'blk', 0,...  14.5 us
    all_to_all x1, blocking collectives, on_device(): lax.all_to_all(partial.reshape(slices, 2, quarter, k), ('z', 'blk'), 0, 0...  14.2 us
    ppermute x1, starting transfers between devices, on_device(): others = lax.ppermute(pieces, 'c', [(i, (i + 1) % nc) for i in range(nc)])  5.3 us
    pallas_call x1, Pallas kernels, on_device(): call(image_kernel, ((2, share, k), BF16), [VMEM] * 2, 'image', 8 * k * or...  4.46 us
    pallas_call x1, Pallas kernels, on_device(): call(left_kernel, ((2, k, share), BF16), [VMEM] * 2, 'left', 8 * k * orde...  4.45 us
  transfers between devices with their start and end apart: 2, of which 1 were waited for; matrix products, arithmetic and copies ran while one was open for 2% of the time, Pallas kernels for 4%

profile of v1, /device:TPU:1, one launch (start us, length us, event | category | flops | bytes accessed | tf_op | source)
XLA Modules:
  0.0 122.8 jit_solution(7726862100238794717)
XLA Ops:
  0.0 0.0 copy-start.3
  0.0 1.1 broadcast_in_dim.14
  1.1 14.5 %all_to_all.20.tile_ref = bf16[4,2,512,128]{3,2,1,0:T(8,128)(2,1)} all-to-all(bf16[4,2,512,128]{3,2,1,0:T(8,128)(2,1)S(1)} %broadcast_in_dim.14), channel_id=1, replica_groups=mesh['sec'=3,'z'=4,'y'=8,'c'=2,'blk'=4] {'blk'}, dimensions={0} | all-to-all | bytes 2097152 | tf_op jit(solution)/shard_map/all_to_all | solution.py:130
  15.6 4.5 %left.1 = bf16[2,128,512]{2,1,0:T(8,128)(2,1)} custom-call(bf16[2,2048,512]{2,1,0:T(8,128)(2,1)} %bitcast.13, bf16[4,2,512,128]{3,2,1,0:T(8,128)(2,1)} %all_to_all.20.tile_ref), custom_call_target="tpu_custom_call" | custom-call | flops 1073741824 | bytes 4194304 | tf_op jit(solution)/shard_map/left/pallas_call | solution.py:133
  20.0 15.1 %collective-permute-start = (bf16[2,128,512]{2,1,0:T(8,128)(2,1)}, bf16[2,128,512]{2,1,0:T(8,128)(2,1)S(1)}, u32[]{:S(2)}, u32[]{:S(2)}) collective-permute-start(bf16[2,128,512]{2,1,0:T(8,128)(2,1)} %left.1), channel_id=1, source_target_pairs={{512,0},{0,256},{256,512},{513,1},{1,257},{257,513},{514,2},{2,258... | collective-permute-start | bytes 786440 | tf_op jit(solution)/shard_map/ppermute | solution.py:136
  35.2 0.0 copy-done.3
  35.2 0.1 copy.7
  35.3 0.1 concatenate.15
  36.0 0.7 fusion.5.refs_2_
  36.7 4.5 %image.1.refs_1_ = bf16[2,512,128]{2,1,0:T(8,128)(2,1)} custom-call(bf16[2,512,2048]{2,1,0:T(8,128)(2,1)} %bitcast.14, bf16[4,2,512,128]{3,2,1,0:T(8,128)(2,1)} %all_to_all.20.tile_ref), custom_call_target="tpu_custom_call" | custom-call | flops 1073741824 | bytes 4194304 | tf_op jit(solution)/shard_map/image/pallas_call | solution.py:137
  41.2 2.9 %collective-permute-done.refs_0_ = bf16[2,128,512]{2,1,0:T(8,128)(2,1)S(1)} collective-permute-done((bf16[2,128,512]{2,1,0:T(8,128)(2,1)}, bf16[2,128,512]{2,1,0:T(8,128)(2,1)S(1)}, u32[]{:S(2)}, u32[]{:S(2)}) %collective-permute-start) | collective-permute-done | bytes 262176 | tf_op jit(solution)/shard_map/ppermute | solution.py:136
  44.0 0.0 copy-start.2
  44.0 0.7 copy-done.2
  44.7 2.0 %pack.1 = bf16[16,48,128]{2,1,0:T(8,128)(2,1)} custom-call(bf16[2,128,512]{2,1,0:T(8,128)(2,1)} %copy-done.2, bf16[2,512,128]{2,1,0:T(8,128)(2,1)} %image.1.refs_1_, bf16[16,128]{1,0:T(8,128)(2,1)} %fusion.5.refs_2_), custom_call_target="tpu_custom_call" | custom-call | tf_op jit(solution)/shard_map/pack/pallas_call | solution.py:143
  46.7 32.3 %all_to_all.21.in_ref = bf16[16,48,128]{2,1,0:T(8,128)(2,1)} all-to-all(bf16[16,48,128]{2,1,0:T(8,128)(2,1)} %pack.1), channel_id=1, replica_groups=mesh['sec'=3,'z'=4,'y'=8,'c'=2,'blk'=4] {'z','blk'}, dimensions={0} | all-to-all | bytes 393216 | tf_op jit(solution)/shard_map/all_to_all | solution.py:149
  79.1 1.6 %sum.1 = bf16[8,4,32,128]{3,2,1,0:T(8,128)(2,1)} custom-call(bf16[16,48,128]{2,1,0:T(8,128)(2,1)} %all_to_all.21.in_ref), custom_call_target="tpu_custom_call" | custom-call | tf_op jit(solution)/shard_map/sum/pallas_call | solution.py:150
  80.7 16.2 %all_to_all.22.refs_1_ = bf16[8,4,32,128]{3,2,1,0:T(8,128)(2,1)S(1)} all-to-all(bf16[8,4,32,128]{3,2,1,0:T(8,128)(2,1)} %sum.1), channel_id=1, replica_groups=mesh['sec'=3,'z'=4,'y'=8,'c'=2,'blk'=4] {'y'}, dimensions={0} | all-to-all | bytes 524288 | tf_op jit(solution)/shard_map/all_to_all | solution.py:151
  97.0 0.0 copy-start
  97.0 5.3 %collective-permute-start.1 = (bf16[8,4,32,128]{3,2,1,0:T(8,128)(2,1)S(1)}, bf16[8,4,32,128]{3,2,1,0:T(8,128)(2,1)S(1)}, u32[]{:S(2)}, u32[]{:S(2)}) collective-permute-start(bf16[8,4,32,128]{3,2,1,0:T(8,128)(2,1)S(1)} %all_to_all.22.refs_1_), channel_id=1, source_target_pairs={{0,4},{4,0},{1,5},{5,1},{2,6},{6,2},{3,7},{7,3},{8,12},{12,8},{9,1... | collective-permute-start | bytes 786440 | tf_op jit(solution)/shard_map/ppermute | solution.py:152
  102.3 0.7 slice.20
  103.0 0.6 convert_select_fusion.refs_0_
  103.6 0.0 collective-permute-done.1.refs_2_
  103.6 0.0 copy-done
  103.6 0.0 copy-start.1
  103.6 0.7 copy-done.1
  104.3 3.6 %product.1 = bf16[4,4,2,32,128]{4,3,2,1,0:T(8,128)(2,1)} custom-call(s32[4,128]{1,0:T(4,128)} %convert_select_fusion.refs_0_, bf16[8,4,32,128]{3,2,1,0:T(8,128)(2,1)} %copy-done, bf16[8,4,32,128]{3,2,1,0:T(8,128)(2,1)} %copy-done.1), custom_call_target="tpu_custom_call" | custom-call | tf_op jit(solution)/shard_map/product/pallas_call | solution.py:157
  107.9 14.2 %all_to_all.23 = bf16[16,2,32,128]{3,2,1,0:T(8,128)(2,1)S(1)} all-to-all(bf16[16,2,32,128]{3,2,1,0:T(8,128)(2,1)} %bitcast.15), channel_id=1, replica_groups=mesh['sec'=3,'z'=4,'y'=8,'c'=2,'blk'=4] {'z','blk'}, dimensions={0} | all-to-all | bytes 524288 | tf_op jit(solution)/shard_map/all_to_all | solution.py:163
  122.1 0.6 multiply_bitcast_fusion
  (3 shorter events, 0.1 us)
Async XLA Ops:
  0.0 35.2 %copy-start.3 = (s32[1,16,2]{1,2,0:T(2,128)S(1)}, s32[1,16,2]{1,2,0:T(2,128)}, u32[]{:S(2)}) copy-start(s32[1,16,2]{1,2,0:T(2,128)} %param.10) | copy-start | bytes 388
  20.0 24.0 %collective-permute-start = (bf16[2,128,512]{2,1,0:T(8,128)(2,1)}, bf16[2,128,512]{2,1,0:T(8,128)(2,1)S(1)}, u32[]{:S(2)}, u32[]{:S(2)}) collective-permute-start(bf16[2,128,512]{2,1,0:T(8,128)(2,1)} %left.1), channel_id=1, source_target_pairs={{512,0},{0,256},{256,512},{513,1},{1,257},{257,513},{514,2},{2,258... | collective-permute-start | bytes 786440 | tf_op jit(solution)/shard_map/ppermute | solution.py:136
  44.0 0.7 copy-start.2
  97.0 6.6 %copy-start = (bf16[8,4,32,128]{3,2,1,0:T(8,128)(2,1)}, bf16[8,4,32,128]{3,2,1,0:T(8,128)(2,1)S(1)}, u32[]{:S(2)}) copy-start(bf16[8,4,32,128]{3,2,1,0:T(8,128)(2,1)S(1)} %all_to_all.22.refs_1_) | copy-start | bytes 786436
  97.0 6.6 %collective-permute-start.1 = (bf16[8,4,32,128]{3,2,1,0:T(8,128)(2,1)S(1)}, bf16[8,4,32,128]{3,2,1,0:T(8,128)(2,1)S(1)}, u32[]{:S(2)}, u32[]{:S(2)}) collective-permute-start(bf16[8,4,32,128]{3,2,1,0:T(8,128)(2,1)S(1)} %all_to_all.22.refs_1_), channel_id=1, source_target_pairs={{0,4},{4,0},{1,5},{5,1},{2,6},{6,2},{3,7},{7,3},{8,12},{12,8},{9,1... | collective-permute-start | bytes 786440 | tf_op jit(solution)/shard_map/ppermute | solution.py:152
  103.6 0.7 copy-start.1

commit v2 on v1

v2 whole, which is shorter than its diff:
```python
import jax
import jax.numpy as jnp
from jax import lax
from jax.experimental import pallas as pl
from jax.experimental.pallas import tpu as pltpu
from jax.sharding import Mesh
from jax.sharding import PartitionSpec as P

TP = ("z", "y", "c")
BF16 = jnp.bfloat16
F32 = jnp.float32
VMEM = pl.BlockSpec(memory_space=pltpu.VMEM)
SMEM = pl.BlockSpec(memory_space=pltpu.SMEM)
HBM = pl.BlockSpec(memory_space=pltpu.HBM)


def dot(a, b, ca, cb):
    return lax.dot_general(a, b, (((ca,), (cb,)), ((), ())), preferred_element_type=F32)


def swapped(x):
    return pltpu.roll(x, x.shape[-1] // 2, x.ndim - 1)


def lower(x):
    return lax.broadcasted_iota(jnp.int32, x.shape, x.ndim - 1) < x.shape[-1] // 2


def halves_kernel(tile_ref, first_ref, second_ref):
    real = tile_ref[0].astype(F32)
    imag = tile_ref[1].astype(F32)
    first_ref[...] = jnp.where(lower(real), real, swapped(imag)).astype(BF16)
    second = jnp.where(lower(real), swapped(real), imag).astype(BF16)
    for j in range(second_ref.shape[0]):
        second_ref[j] = second


def copies_kernel(own_ref, other_ref, out_ref):
    own, other = own_ref[...], other_ref[...]
    for j in range(out_ref.shape[0]):
        out_ref[j, 0] = own
        out_ref[j, 1] = other


def chunked(source, target, sems, dim, size):
    copies = []
    for j in range(source.shape[dim] // size):
        at = tuple(pl.ds(j * size, size) if d == dim else slice(None) for d in range(3))
        copies.append(pltpu.make_async_copy(source.at[at], target.at[at], sems.at[j]))
        copies[-1].start()
    return copies


def left_half(tile_of, beta_ref, copies):
    acc_r = acc_i = None
    for j, copy in enumerate(copies):
        copy.wait()
        tile = tile_of(j)
        rows = tile.shape[0]
        add_r = dot(tile, beta_ref[0, j * rows : (j + 1) * rows, :], 0, 0)
        add_i = dot(tile, beta_ref[1, j * rows : (j + 1) * rows, :], 0, 0)
        acc_r = add_r if acc_r is None else acc_r + add_r
        acc_i = add_i if acc_i is None else acc_i + add_i
    h = acc_r.shape[0] // 2
    return acc_r[:h] + acc_i[h:], acc_i[:h] - acc_r[h:]


def left_kernel(beta_hbm, tile_ref, left_ref, beta_ref, sems):
    copies = chunked(beta_hbm, beta_ref, sems, 1, tile_ref.shape[1])
    real, imag = left_half(lambda j: tile_ref[j], beta_ref, copies)
    left_ref[0] = real.astype(BF16)
    left_ref[1] = imag.astype(BF16)


def middle_kernel(
    tau_hbm, beta_hbm, first_ref, second_ref, left_ref, image_ref, beta_ref, tau_ref, sems
):
    parts, _, rows, k = first_ref.shape
    beta_copies = chunked(beta_hbm, beta_ref, sems.at[0], 1, rows)
    tau_copies = chunked(tau_hbm, tau_ref, sems.at[1], 2, rows)
    real, imag = left_half(lambda j: first_ref[j, 1], beta_ref, beta_copies)
    left_ref[0] = real.astype(BF16)
    left_ref[1] = imag.astype(BF16)
    acc_r = acc_i = None
    for j in range(parts):
        tau_copies[j].wait()
        both = jnp.concatenate([first_ref[j, 0], second_ref[j]], axis=1)
        add_r = dot(tau_ref[0, :, j * rows : (j + 1) * rows], both, 1, 0)
        add_i = dot(tau_ref[1, :, j * rows : (j + 1) * rows], both, 1, 0)
        acc_r = add_r if acc_r is None else acc_r + add_r
        acc_i = add_i if acc_i is None else acc_i + add_i
    for h in range(2):
        a, b = acc_r[:, h * k : (h + 1) * k], swapped(acc_i[:, h * k : (h + 1) * k])
        image_ref[:, h * k : (h + 1) * k] = (a + jnp.where(lower(b), -b, b)).astype(BF16)


def pack_kernel(scale, lists_ref, load_ref, first_ref, second_ref, image_ref, out_ref):
    slices = out_ref.shape[0]
    k = image_ref.shape[1] // 2
    image = image_ref[...]
    from_r = dot(jnp.concatenate([first_ref[0], second_ref[0]], axis=0), image, 1, 0)
    from_i = dot(jnp.concatenate([first_ref[1], second_ref[1]], axis=0), image, 1, 0)
    halves = []
    for h in range(2):
        a, b = from_r[:, h * k : (h + 1) * k], swapped(from_i[:, h * k : (h + 1) * k])
        halves.append(a + jnp.where(lower(b), -b, b))
    first, second = halves
    real = jnp.where(lower(first), first, swapped(second)) * scale
    imag = jnp.where(lower(first), swapped(first), second) * scale
    cut = [x.reshape(slices, k // slices, k) for x in (real.T, imag.T, real, imag)]
    packed = jnp.concatenate(cut, axis=1).astype(BF16)
    n = packed.shape[1]
    out_ref[:, :n, :] = packed
    sides, slots = lists_ref.shape
    row = lax.broadcasted_iota(jnp.int32, (out_ref.shape[1] - n, k), 0)
    column = lax.broadcasted_iota(jnp.int32, row.shape, 1)
    meta = jnp.where(row == sides, load_ref[0], 0)
    for side in range(sides):
        for g in range(slots):
            meta = jnp.where((row == side) & (column == g), lists_ref[side, g], meta)
    meta = meta.astype(F32).astype(BF16)
    for j in range(slices):
        out_ref[j, n:, :] = meta


def sum_kernel(in_ref, out_ref, numbers_ref):
    copies, pairs, rows, _ = out_ref.shape
    parts = in_ref.shape[0] // pairs
    tail = numbers_ref.shape[1]
    for q in range(pairs):
        total = in_ref[q * parts, :rows, :].astype(F32)
        for j in range(1, parts):
            total = total + in_ref[q * parts + j, :rows, :].astype(F32)
        total = total.astype(BF16)
        for y in range(copies):
            out_ref[y, q] = total
        numbers_ref[q] = in_ref[q * parts, rows:, :].astype(F32).astype(jnp.int32)[:tail]


def product_kernel(slots, ny, nc, scale, numbers_ref, own_ref, other_ref, out_ref):
    owners, quarters, _, rows, k = out_ref.shape
    w = own_ref.shape[2] // 4
    mine = lax.axis_index("c")
    for o in range(owners):
        load = numbers_ref[o, 2, 0]

        def fetch(p, at):
            z = p // (ny * nc)
            y = (p // nc) % ny
            here = own_ref[y, z, at : at + 2 * w, :]
            there = other_ref[y, z, at : at + 2 * w, :]
            return jnp.where((p % nc) == mine, here, there)

        lefts, reals, imags = [], [], []
        for g in range(slots):
            left = fetch(numbers_ref[o, 0, g], 0)
            right = fetch(numbers_ref[o, 1, g], 2 * w).astype(F32)
            lefts.append(jnp.where(g < load, left, jnp.zeros_like(left)))
            reals += [right[:w], -right[w:]]
            imags += [right[w:], right[:w]]
        left = jnp.concatenate(lefts, axis=0)
        right = jnp.concatenate(
            [jnp.concatenate(reals, axis=0), jnp.concatenate(imags, axis=0)], axis=1
        ).astype(BF16)
        both = dot(left, right, 0, 0) * scale
        for q in range(quarters):
            for c in range(2):
                out_ref[o, q, c] = both[q * rows : (q + 1) * rows, c * k : (c + 1) * k].astype(BF16)


def call(kernel, outs, specs, name, scratch=(), flops=0, moved=0, grant=16):
    outs = [jax.ShapeDtypeStruct(*out) for out in outs]
    return pl.pallas_call(
        kernel,
        out_shape=outs,
        in_specs=specs,
        out_specs=[VMEM] * len(outs),
        scratch_shapes=scratch,
        name=name,
        compiler_params=pltpu.CompilerParams(vmem_limit_bytes=grant * 2**20),
        cost_estimate=pl.CostEstimate(flops=flops, bytes_accessed=moved, transcendentals=0),
    )


def on_device(perambulator, backward, elementals, diagrams, owner_loads):
    tau = pltpu.with_memory_space_constraint(perambulator[0], pltpu.HBM)
    beta = pltpu.with_memory_space_constraint(backward[0], pltpu.HBM)
    tile = elementals[0, 0]
    _, share, k = tile.shape
    order = tau.shape[2]
    nx, nz, ny, nc = (lax.axis_size(a) for a in ("blk", "z", "y", "c"))
    ns = lax.axis_size("sec")
    slots = diagrams.shape[1]
    slices = nz * nx
    w = k // slices
    quarter = k // nx
    onward = [((i - 1) % ns, i) for i in range(ns)]
    work = 4 * k * order * share

    first, second = call(
        halves_kernel, [((share, k), BF16), ((nx, share, k), BF16)], [VMEM], "halves"
    )(tile)
    first_before = lax.ppermute(first, "sec", onward)
    seconds = lax.all_to_all(second, "blk", 0, 0, tiled=True)
    (left_second,) = call(
        left_kernel,
        [((2, k // 2, share), BF16)],
        [HBM, VMEM],
        "left",
        [pltpu.VMEM(beta.shape, BF16), pltpu.SemaphoreType.DMA((nx,))],
        work,
        2**22,
        16,
    )(beta, seconds)
    left_second = lax.ppermute(left_second, "sec", onward)
    (copies,) = call(copies_kernel, [((nx, 2, share, k), BF16)], [VMEM] * 2, "copies")(
        first, first_before
    )
    firsts = lax.all_to_all(copies, "blk", 0, 0, tiled=True)
    left_first, image = call(
        middle_kernel,
        [((2, k // 2, share), BF16), ((share, 2 * k), BF16)],
        [HBM, HBM, VMEM, VMEM],
        "middle",
        [
            pltpu.VMEM(beta.shape, BF16),
            pltpu.VMEM(tau.shape, BF16),
            pltpu.SemaphoreType.DMA((2, nx)),
        ],
        3 * work,
        2**23,
        16,
    )(tau, beta, firsts, seconds)

    (packed,) = call(
        lambda *refs: pack_kernel(order**-0.5, *refs),
        [((slices, 4 * w + 16, k), BF16)],
        [SMEM, SMEM, VMEM, VMEM, VMEM],
        "pack",
    )(diagrams[0].T, owner_loads, left_first, left_second, image)
    packed = lax.all_to_all(packed, ("z", "blk"), 0, 0, tiled=True)
    pieces, numbers = call(
        sum_kernel,
        [((ny, nz, 4 * w, k), BF16), ((nz, 8, k), jnp.int32)],
        [VMEM],
        "sum",
    )(packed)
    pieces = lax.all_to_all(pieces, "y", 0, 0, tiled=True)
    others = lax.ppermute(pieces, "c", [(i, (i + 1) % nc) for i in range(nc)])
    (partial,) = call(
        lambda *refs: product_kernel(slots, ny, nc, (k * slots) ** -0.5, *refs),
        [((nz, nx, 2, quarter, k), BF16)],
        [SMEM, VMEM, VMEM],
        "product",
    )(numbers, pieces, others)
    arrived = lax.all_to_all(
        partial.reshape(slices, 2, quarter, k), ("z", "blk"), 0, 0, tiled=True
    )
    total = jnp.sum(arrived.astype(F32), axis=0)
    return total.reshape(1, 1, 2, quarter, k)


def solution(mesh):
    torus = Mesh(
        mesh.devices.reshape(mesh.shape["sec"], 4, 8, 2, mesh.shape["blk"]),
        ("sec", "z", "y", "c", "blk"),
    )
    in_specs = (
        P(TP, None, "blk", None),
        P(TP, None, None, "blk"),
        P("sec", TP, None, "blk", None),
        P(TP, None, None),
        P(TP),
    )
    out_specs = P("sec", TP, None, "blk", None)
    return jax.shard_map(
        on_device, mesh=torus, in_specs=in_specs, out_specs=out_specs, check_vma=False
    )
```

time: 123 us -> 111 us (0.902)
  blocking collectives: 77.3 us -> 54.7 us
  starting transfers between devices: 20.4 us -> 30.3 us
  waiting for transfers between devices: 2.88 us -> 11.1 us
  Pallas kernels: 16.1 us -> 12.6 us
  local copies, waits for them, and re-layouts: 3.38 us -> 0.95 us
  other arithmetic: 1.93 us -> 0.66 us
    all_to_all x1 -> x0, blocking collectives: 14.5 us -> none  [on_device(): lax.all_to_all(jnp.broadcast_to(tile[None], (nx, *tile.shape)), 'blk', 0,...]
    all_to_all x0 -> x2, starting transfers between devices: none -> 9.07 us  [the longest x1 4.83 us: on_device(): seconds = lax.all_to_all(second, 'blk', 0, 0, tiled=True)]
    all_to_all x1, blocking collectives: 32.3 us -> 26 us  [on_device(): packed = lax.all_to_all(packed, ('z', 'blk'), 0, 0, tiled=True)]
    all_to_all x0 -> x2, waiting for transfers between devices: none -> 3.7 us  [the longest x1 3.7 us: on_device(): firsts = lax.all_to_all(copies, 'blk', 0, 0, tiled=True)]
    pallas_call x5 -> x7, Pallas kernels: 16.1 us -> 12.6 us  [the longest x1 4.32 us: on_device(): call(middle_kernel, [((2, k // 2, share), BF16), ((share, 2 * k), BF16)],...]
    ppermute x1 -> x2, waiting for transfers between devices: 2.88 us -> 6.28 us  [the longest x1 6.28 us: on_device(): first_before = lax.ppermute(first, 'sec', onward)]
    all_to_all x1, blocking collectives: 14.2 us -> 12.7 us  [on_device(): lax.all_to_all(partial.reshape(slices, 2, quarter, k), ('z', 'blk'), 0, 0...]
    ppermute x1 -> x2, starting transfers between devices: 15.1 us -> 14.9 us  [the longest x1 10.6 us: on_device(): first_before = lax.ppermute(first, 'sec', onward)]
  transfers between devices with their start and end apart: 2 -> 5, of which waited for: 1 -> 3; matrix products, arithmetic and copies ran while one was open for 2% -> 0% of each run, Pallas kernels for 4% -> 7%
where the time goes in v2:
time: 111 us
  blocking collectives  54.7 us (49%)
  starting transfers between devices  30.3 us (27%)
  Pallas kernels  12.6 us (11%)
  waiting for transfers between devices  11.1 us (10%)
    all_to_all x1, blocking collectives, on_device(): packed = lax.all_to_all(packed, ('z', 'blk'), 0, 0, tiled=True)  26 us
    all_to_all x1, blocking collectives, on_device(): pieces = lax.all_to_all(pieces, 'y', 0, 0, tiled=True)  16.1 us
    all_to_all x1, blocking collectives, on_device(): lax.all_to_all(partial.reshape(slices, 2, quarter, k), ('z', 'blk'), 0, 0...  12.7 us
    ppermute x1, starting transfers between devices, on_device(): first_before = lax.ppermute(first, 'sec', onward)  10.6 us
    ppermute x1, starting transfers between devices, on_device(): others = lax.ppermute(pieces, 'c', [(i, (i + 1) % nc) for i in range(nc)])  6.28 us
    ppermute x1, waiting for transfers between devices, on_device(): first_before = lax.ppermute(first, 'sec', onward)  6.28 us
    all_to_all x1, starting transfers between devices, on_device(): seconds = lax.all_to_all(second, 'blk', 0, 0, tiled=True)  4.83 us
    pallas_call x1, Pallas kernels, on_device(): call(middle_kernel, [((2, k // 2, share), BF16), ((share, 2 * k), BF16)],...  4.32 us
  transfers between devices with their start and end apart: 5, of which 3 were waited for; matrix products, arithmetic and copies ran while one was open for 0% of the time, Pallas kernels for 7%

profile of v2, /device:TPU:1, one launch (start us, length us, event | category | flops | bytes accessed | tf_op | source)
XLA Modules:
  0.0 111.0 jit_solution(4818939959509817092)
XLA Ops:
  0.0 0.0 copy-start
  0.0 0.9 copy-done
  1.0 1.0 halves.1
  1.9 4.8 %all-to-all-start.1 = ((bf16[4,512,128]{2,1,0:T(8,128)(2,1)}), bf16[4,512,128]{2,1,0:T(8,128)(2,1)S(1)}, u32[]{:S(2)}, u32[]{:S(2)}) async-start(bf16[4,512,128]{2,1,0:T(8,128)(2,1)} %get-tuple-element.12), calls=%async_computation.1 | async-start | bytes 1048576 | tf_op jit(solution)/shard_map/all_to_all | solution.py:204
  6.7 10.6 %collective-permute-start = (bf16[512,128]{1,0:T(8,128)(2,1)S(1)}, bf16[512,128]{1,0:T(8,128)(2,1)S(1)}, u32[]{:S(2)}, u32[]{:S(2)}) collective-permute-start(bf16[512,128]{1,0:T(8,128)(2,1)S(1)} %get-tuple-element.11.own_ref), channel_id=1, source_target_pairs={{512,0},{0,256},{256,512},{513,1},{1,257},{257,513},{514,2},{2,258... | collective-permute-start | bytes 393224 | tf_op jit(solution)/shard_map/ppermute | solution.py:203
  17.4 6.3 %collective-permute-done.other_ref = bf16[512,128]{1,0:T(8,128)(2,1)S(1)} collective-permute-done((bf16[512,128]{1,0:T(8,128)(2,1)S(1)}, bf16[512,128]{1,0:T(8,128)(2,1)S(1)}, u32[]{:S(2)}, u32[]{:S(2)}) %collective-permute-start) | collective-permute-done | bytes 131104 | tf_op jit(solution)/shard_map/ppermute | solution.py:203
  23.7 1.1 copies.1
  24.8 0.0 all-to-all-done.1.second_ref.tile_ref
  24.8 4.2 %all-to-all-start = ((bf16[4,2,512,128]{3,2,1,0:T(8,128)(2,1)}), bf16[4,2,512,128]{3,2,1,0:T(8,128)(2,1)S(1)}, u32[]{:S(2)}, u32[]{:S(2)}) async-start(bf16[4,2,512,128]{3,2,1,0:T(8,128)(2,1)} %copies.1), calls=%async_computation | async-start | bytes 2097152 | tf_op jit(solution)/shard_map/all_to_all | solution.py:219
  29.6 2.5 %left.1 = bf16[2,64,512]{2,1,0:T(8,128)(2,1)S(1)} custom-call(bf16[2,2048,512]{2,1,0:T(8,128)(2,1)} %bitcast.11, bf16[4,512,128]{2,1,0:T(8,128)(2,1)S(1)} %all-to-all-done.1.second_ref.tile_ref), custom_call_target="tpu_custom_call" | custom-call | flops 536870912 | bytes 4194304 | tf_op jit(solution)/shard_map/left/pallas_call | solution.py:205
  32.2 4.3 %collective-permute-start.1 = (bf16[2,64,512]{2,1,0:T(8,128)(2,1)S(1)}, bf16[2,64,512]{2,1,0:T(8,128)(2,1)S(1)}, u32[]{:S(2)}, u32[]{:S(2)}) collective-permute-start(bf16[2,64,512]{2,1,0:T(8,128)(2,1)S(1)} %left.1), channel_id=1, source_target_pairs={{512,0},{0,256},{256,512},{513,1},{1,257},{257,513},{514,2},{2,258... | collective-permute-start | bytes 393224 | tf_op jit(solution)/shard_map/ppermute | solution.py:215
  36.5 3.7 %all-to-all-done.first_ref = bf16[4,2,512,128]{3,2,1,0:T(8,128)(2,1)S(1)} async-done(((bf16[4,2,512,128]{3,2,1,0:T(8,128)(2,1)}), bf16[4,2,512,128]{3,2,1,0:T(8,128)(2,1)S(1)}, u32[]{:S(2)}, u32[]{:S(2)}) %all-to-all-start) | async-done | bytes 1048608 | tf_op jit(solution)/shard_map/all_to_all | solution.py:219
  40.2 0.0 copy-start.1
  40.2 4.3 %middle.1 = (bf16[2,64,512]{2,1,0:T(8,128)(2,1)S(1)}, bf16[512,256]{1,0:T(8,128)(2,1)S(1)}) custom-call(bf16[2,512,2048]{2,1,0:T(8,128)(2,1)} %bitcast.13, bf16[2,2048,512]{2,1,0:T(8,128)(2,1)} %bitcast.12, bf16[4,2,512,128]{3,2,1,0:T(8,128)(2,1)S(1)} %all-to-all-done.first_ref, bf16[4,512,128]{2,1,0:T(8,128)(2,1)S(1)} %all-to-all-done.1.second_ref.tile_ref), custom_call_target="tpu_custom_call" | custom-call | flops 1610612736 | bytes 8388608 | tf_op jit(solution)/shard_map/middle/pallas_call | solution.py:220
  44.5 0.0 collective-permute-done.1.refs_3_
  44.5 0.0 copy-done.1
  44.5 1.0 pack.1
  45.5 26.0 %all_to_all.25.in_ref = bf16[16,48,128]{2,1,0:T(8,128)(2,1)S(1)} all-to-all(bf16[16,48,128]{2,1,0:T(8,128)(2,1)S(1)} %pack.1), channel_id=1, replica_groups=mesh['sec'=3,'z'=4,'y'=8,'c'=2,'blk'=4] {'z','blk'}, dimensions={0} | all-to-all | bytes 393216 | tf_op jit(solution)/shard_map/all_to_all | solution.py:241
  71.6 16.1 %all_to_all.26.refs_1_ = bf16[8,4,32,128]{3,2,1,0:T(8,128)(2,1)S(1)} all-to-all(bf16[8,4,32,128]{3,2,1,0:T(8,128)(2,1)S(1)} %get-tuple-element.16), channel_id=1, replica_groups=mesh['sec'=3,'z'=4,'y'=8,'c'=2,'blk'=4] {'y'}, dimensions={0} | all-to-all | bytes 524288 | tf_op jit(solution)/shard_map/all_to_all | solution.py:248
  87.7 6.3 %collective-permute-start.2 = (bf16[8,4,32,128]{3,2,1,0:T(8,128)(2,1)S(1)}, bf16[8,4,32,128]{3,2,1,0:T(8,128)(2,1)S(1)}, u32[]{:S(2)}, u32[]{:S(2)}) collective-permute-start(bf16[8,4,32,128]{3,2,1,0:T(8,128)(2,1)S(1)} %all_to_all.26.refs_1_), channel_id=1, source_target_pairs={{0,4},{4,0},{1,5},{5,1},{2,6},{6,2},{3,7},{7,3},{8,12},{12,8},{9,1... | collective-permute-start | bytes 786440 | tf_op jit(solution)/shard_map/ppermute | solution.py:249
  93.9 1.1 %collective-permute-done.2.refs_2_ = bf16[8,4,32,128]{3,2,1,0:T(8,128)(2,1)S(1)} collective-permute-done((bf16[8,4,32,128]{3,2,1,0:T(8,128)(2,1)S(1)}, bf16[8,4,32,128]{3,2,1,0:T(8,128)(2,1)S(1)}, u32[]{:S(2)}, u32[]{:S(2)}) %collective-permute-start.2) | collective-permute-done | bytes 262176 | tf_op jit(solution)/shard_map/ppermute | solution.py:249
  95.1 2.6 %product.1 = bf16[4,4,2,32,128]{4,3,2,1,0:T(8,128)(2,1)S(1)} custom-call(s32[4,8,128]{2,1,0:T(8,128)S(1)} %get-tuple-element.15.refs_0_, bf16[8,4,32,128]{3,2,1,0:T(8,128)(2,1)S(1)} %all_to_all.26.refs_1_, bf16[8,4,32,128]{3,2,1,0:T(8,128)(2,1)S(1)} %collective-permute-done.2.refs_2_), custom_call_target="tpu_custom_call" | custom-call | tf_op jit(solution)/shard_map/product/pallas_call | solution.py:250
  97.7 12.7 %all_to_all.27 = bf16[16,2,32,128]{3,2,1,0:T(8,128)(2,1)S(1)} all-to-all(bf16[16,2,32,128]{3,2,1,0:T(8,128)(2,1)S(1)} %bitcast.8), channel_id=1, replica_groups=mesh['sec'=3,'z'=4,'y'=8,'c'=2,'blk'=4] {'z','blk'}, dimensions={0} | all-to-all | bytes 524288 | tf_op jit(solution)/shard_map/all_to_all | solution.py:256
  110.4 0.7 convert_reduce_fusion
  (1 shorter events, 0.0 us)
Async XLA Ops:
  0.0 0.9 copy-start
  1.9 22.8 %all-to-all-start.1 = ((bf16[4,512,128]{2,1,0:T(8,128)(2,1)}), bf16[4,512,128]{2,1,0:T(8,128)(2,1)S(1)}, u32[]{:S(2)}, u32[]{:S(2)}) async-start(bf16[4,512,128]{2,1,0:T(8,128)(2,1)} %get-tuple-element.12), calls=%async_computation.1 | async-start | bytes 1048576 | tf_op jit(solution)/shard_map/all_to_all | solution.py:204
  6.7 16.9 %collective-permute-start = (bf16[512,128]{1,0:T(8,128)(2,1)S(1)}, bf16[512,128]{1,0:T(8,128)(2,1)S(1)}, u32[]{:S(2)}, u32[]{:S(2)}) collective-permute-start(bf16[512,128]{1,0:T(8,128)(2,1)S(1)} %get-tuple-element.11.own_ref), channel_id=1, source_target_pairs={{512,0},{0,256},{256,512},{513,1},{1,257},{257,513},{514,2},{2,258... | collective-permute-start | bytes 393224 | tf_op jit(solution)/shard_map/ppermute | solution.py:203
  24.8 15.4 %all-to-all-start = ((bf16[4,2,512,128]{3,2,1,0:T(8,128)(2,1)}), bf16[4,2,512,128]{3,2,1,0:T(8,128)(2,1)S(1)}, u32[]{:S(2)}, u32[]{:S(2)}) async-start(bf16[4,2,512,128]{3,2,1,0:T(8,128)(2,1)} %copies.1), calls=%async_computation | async-start | bytes 2097152 | tf_op jit(solution)/shard_map/all_to_all | solution.py:219
  32.2 12.3 %collective-permute-start.1 = (bf16[2,64,512]{2,1,0:T(8,128)(2,1)S(1)}, bf16[2,64,512]{2,1,0:T(8,128)(2,1)S(1)}, u32[]{:S(2)}, u32[]{:S(2)}) collective-permute-start(bf16[2,64,512]{2,1,0:T(8,128)(2,1)S(1)} %left.1), channel_id=1, source_target_pairs={{512,0},{0,256},{256,512},{513,1},{1,257},{257,513},{514,2},{2,258... | collective-permute-start | bytes 393224 | tf_op jit(solution)/shard_map/ppermute | solution.py:215
  40.2 4.3 %copy-start.1 = (s32[1,16,2]{1,2,0:T(2,128)S(1)}, s32[1,16,2]{1,2,0:T(2,128)}, u32[]{:S(2)}) copy-start(s32[1,16,2]{1,2,0:T(2,128)} %param.8) | copy-start | bytes 388
  87.7 7.4 %collective-permute-start.2 = (bf16[8,4,32,128]{3,2,1,0:T(8,128)(2,1)S(1)}, bf16[8,4,32,128]{3,2,1,0:T(8,128)(2,1)S(1)}, u32[]{:S(2)}, u32[]{:S(2)}) collective-permute-start(bf16[8,4,32,128]{3,2,1,0:T(8,128)(2,1)S(1)} %all_to_all.26.refs_1_), channel_id=1, source_target_pairs={{0,4},{4,0},{1,5},{5,1},{2,6},{6,2},{3,7},{7,3},{8,12},{12,8},{9,1... | collective-permute-start | bytes 786440 | tf_op jit(solution)/shard_map/ppermute | solution.py:249

commit v3 on v2

--- a/solution.py
+++ b/solution.py
@@ -6,11 +6,13 @@
 from jax.sharding import Mesh
 from jax.sharding import PartitionSpec as P
 
+
 TP = ("z", "y", "c")
 BF16 = jnp.bfloat16
 F32 = jnp.float32
 VMEM = pl.BlockSpec(memory_space=pltpu.VMEM)
 SMEM = pl.BlockSpec(memory_space=pltpu.SMEM)
+ANY = pl.BlockSpec(memory_space=pl.ANY)
 HBM = pl.BlockSpec(memory_space=pltpu.HBM)
 
 
@@ -35,7 +37,7 @@
         second_ref[j] = second
 
 
-def copies_kernel(own_ref, other_ref, out_ref):
+def copies_kernel(own_ref, other_ref, _, out_ref):
     own, other = own_ref[...], other_ref[...]
     for j in range(out_ref.shape[0]):
         out_ref[j, 0] = own
@@ -168,7 +170,7 @@
                 out_ref[o, q, c] = both[q * rows : (q + 1) * rows, c * k : (c + 1) * k].astype(BF16)
 
 
-def call(kernel, outs, specs, name, scratch=(), flops=0, moved=0, grant=16):
+def call(kernel, outs, specs, scratch=(), flops=0, moved=0, grant=16):
     outs = [jax.ShapeDtypeStruct(*out) for out in outs]
     return pl.pallas_call(
         kernel,
@@ -176,7 +178,6 @@
         in_specs=specs,
         out_specs=[VMEM] * len(outs),
         scratch_shapes=scratch,
-        name=name,
         compiler_params=pltpu.CompilerParams(vmem_limit_bytes=grant * 2**20),
         cost_estimate=pl.CostEstimate(flops=flops, bytes_accessed=moved, transcendentals=0),
     )
@@ -197,31 +198,27 @@
     onward = [((i - 1) % ns, i) for i in range(ns)]
     work = 4 * k * order * share
 
-    first, second = call(
-        halves_kernel, [((share, k), BF16), ((nx, share, k), BF16)], [VMEM], "halves"
-    )(tile)
+    first, second = call(halves_kernel, [((share, k), BF16), ((nx, share, k), BF16)], [VMEM])(tile)
     first_before = lax.ppermute(first, "sec", onward)
     seconds = lax.all_to_all(second, "blk", 0, 0, tiled=True)
     (left_second,) = call(
         left_kernel,
         [((2, k // 2, share), BF16)],
         [HBM, VMEM],
-        "left",
         [pltpu.VMEM(beta.shape, BF16), pltpu.SemaphoreType.DMA((nx,))],
         work,
         2**22,
         16,
     )(beta, seconds)
-    left_second = lax.ppermute(left_second, "sec", onward)
-    (copies,) = call(copies_kernel, [((nx, 2, share, k), BF16)], [VMEM] * 2, "copies")(
-        first, first_before
+    left_before = lax.ppermute(left_second, "sec", onward)
+    (copies,) = call(copies_kernel, [((nx, 2, share, k), BF16)], [VMEM, VMEM, ANY])(
+        first, first_before, left_second
     )
     firsts = lax.all_to_all(copies, "blk", 0, 0, tiled=True)
     left_first, image = call(
         middle_kernel,
         [((2, k // 2, share), BF16), ((share, 2 * k), BF16)],
         [HBM, HBM, VMEM, VMEM],
-        "middle",
         [
             pltpu.VMEM(beta.shape, BF16),
             pltpu.VMEM(tau.shape, BF16),
@@ -236,14 +233,10 @@
         lambda *refs: pack_kernel(order**-0.5, *refs),
         [((slices, 4 * w + 16, k), BF16)],
         [SMEM, SMEM, VMEM, VMEM, VMEM],
-        "pack",
-    )(diagrams[0].T, owner_loads, left_first, left_second, image)
+    )(diagrams[0].T, owner_loads, left_first, left_before, image)
     packed = lax.all_to_all(packed, ("z", "blk"), 0, 0, tiled=True)
     pieces, numbers = call(
-        sum_kernel,
-        [((ny, nz, 4 * w, k), BF16), ((nz, 8, k), jnp.int32)],
-        [VMEM],
-        "sum",
+        sum_kernel, [((ny, nz, 4 * w, k), BF16), ((nz, 8, k), jnp.int32)], [VMEM]
     )(packed)
     pieces = lax.all_to_all(pieces, "y", 0, 0, tiled=True)
     others = lax.ppermute(pieces, "c", [(i, (i + 1) % nc) for i in range(nc)])
@@ -251,7 +244,6 @@
         lambda *refs: product_kernel(slots, ny, nc, (k * slots) ** -0.5, *refs),
         [((nz, nx, 2, quarter, k), BF16)],
         [SMEM, VMEM, VMEM],
-        "product",
     )(numbers, pieces, others)
     arrived = lax.all_to_all(
         partial.reshape(slices, 2, quarter, k), ("z", "blk"), 0, 0, tiled=True

time: 111 us -> 111 us (level)
    ppermute x1, waiting for transfers between devices: 6.28 us -> 3.72 us  [on_device(): first_before = lax.ppermute(first, 'sec', onward)]
    all_to_all x1, waiting for transfers between devices: 3.7 us -> 6 us  [on_device(): firsts = lax.all_to_all(copies, 'blk', 0, 0, tiled=True)]
  transfers between devices with their start and end apart: 5 -> 5, of which waited for: 3 -> 3; matrix products, arithmetic and copies ran while one was open for 0% -> 0% of each run, Pallas kernels for 7% -> 6%
where the time goes in v3:
time: 111 us
  blocking collectives  54.7 us (49%)
  starting transfers between devices  30.5 us (27%)
  Pallas kernels  12.6 us (11%)
  waiting for transfers between devices  10.9 us (10%)
    all_to_all x1, blocking collectives, on_device(): packed = lax.all_to_all(packed, ('z', 'blk'), 0, 0, tiled=True)  26 us
    all_to_all x1, blocking collectives, on_device(): pieces = lax.all_to_all(pieces, 'y', 0, 0, tiled=True)  16.1 us
    all_to_all x1, blocking collectives, on_device(): lax.all_to_all(partial.reshape(slices, 2, quarter, k), ('z', 'blk'), 0, 0...  12.7 us
    ppermute x1, starting transfers between devices, on_device(): first_before = lax.ppermute(first, 'sec', onward)  10.6 us
    ppermute x1, starting transfers between devices, on_device(): others = lax.ppermute(pieces, 'c', [(i, (i + 1) % nc) for i in range(nc)])  6.28 us
    all_to_all x1, waiting for transfers between devices, on_device(): firsts = lax.all_to_all(copies, 'blk', 0, 0, tiled=True)  6 us
    all_to_all x1, starting transfers between devices, on_device(): seconds = lax.all_to_all(second, 'blk', 0, 0, tiled=True)  4.83 us
    ppermute x1, starting transfers between devices, on_device(): left_before = lax.ppermute(left_second, 'sec', onward)  4.53 us
  transfers between devices with their start and end apart: 5, of which 3 were waited for; matrix products, arithmetic and copies ran while one was open for 0% of the time, Pallas kernels for 6%

profile of v3, /device:TPU:1, one launch (start us, length us, event | category | flops | bytes accessed | tf_op | source)
XLA Modules:
  0.0 111.0 jit_solution(17953280551739677778)
XLA Ops:
  0.0 0.0 copy-start
  0.0 0.9 copy-done
  1.0 0.9 shard_map.55
  1.9 4.8 %all-to-all-start = ((bf16[4,512,128]{2,1,0:T(8,128)(2,1)}), bf16[4,512,128]{2,1,0:T(8,128)(2,1)S(1)}, u32[]{:S(2)}, u32[]{:S(2)}) async-start(bf16[4,512,128]{2,1,0:T(8,128)(2,1)} %get-tuple-element.12), calls=%async_computation | async-start | bytes 1048576 | tf_op jit(solution)/shard_map/all_to_all | solution.py:203
  6.7 10.6 %collective-permute-start = (bf16[512,128]{1,0:T(8,128)(2,1)S(1)}, bf16[512,128]{1,0:T(8,128)(2,1)S(1)}, u32[]{:S(2)}, u32[]{:S(2)}) collective-permute-start(bf16[512,128]{1,0:T(8,128)(2,1)S(1)} %get-tuple-element.11.own_ref), channel_id=1, source_target_pairs={{512,0},{0,256},{256,512},{513,1},{1,257},{257,513},{514,2},{2,258... | collective-permute-start | bytes 393224 | tf_op jit(solution)/shard_map/ppermute | solution.py:202
  17.4 0.0 all-to-all-done.tile_ref.second_ref
  17.4 2.5 %shard_map.56._ = bf16[2,64,512]{2,1,0:T(8,128)(2,1)S(1)} custom-call(bf16[2,2048,512]{2,1,0:T(8,128)(2,1)} %bitcast.11, bf16[4,512,128]{2,1,0:T(8,128)(2,1)S(1)} %all-to-all-done.tile_ref.second_ref), custom_call_target="tpu_custom_call" | custom-call | flops 536870912 | bytes 4194304 | tf_op jit(solution)/shard_map/pallas_call | solution.py:204
  19.9 3.7 %collective-permute-done.other_ref = bf16[512,128]{1,0:T(8,128)(2,1)S(1)} collective-permute-done((bf16[512,128]{1,0:T(8,128)(2,1)S(1)}, bf16[512,128]{1,0:T(8,128)(2,1)S(1)}, u32[]{:S(2)}, u32[]{:S(2)}) %collective-permute-start) | collective-permute-done | bytes 131104 | tf_op jit(solution)/shard_map/ppermute | solution.py:202
  23.6 1.1 shard_map.57
  24.7 4.2 %all-to-all-start.1 = ((bf16[4,2,512,128]{3,2,1,0:T(8,128)(2,1)}), bf16[4,2,512,128]{3,2,1,0:T(8,128)(2,1)S(1)}, u32[]{:S(2)}, u32[]{:S(2)}) async-start(bf16[4,2,512,128]{3,2,1,0:T(8,128)(2,1)} %shard_map.57), calls=%async_computation.1 | async-start | bytes 2097152 | tf_op jit(solution)/shard_map/all_to_all | solution.py:217
  29.6 4.5 %collective-permute-start.1 = (bf16[2,64,512]{2,1,0:T(8,128)(2,1)S(1)}, bf16[2,64,512]{2,1,0:T(8,128)(2,1)S(1)}, u32[]{:S(2)}, u32[]{:S(2)}) collective-permute-start(bf16[2,64,512]{2,1,0:T(8,128)(2,1)S(1)} %shard_map.56._), channel_id=1, source_target_pairs={{512,0},{0,256},{256,512},{513,1},{1,257},{257,513},{514,2},{2,258... | collective-permute-start | bytes 393224 | tf_op jit(solution)/shard_map/ppermute | solution.py:213
  34.2 6.0 %all-to-all-done.1.first_ref = bf16[4,2,512,128]{3,2,1,0:T(8,128)(2,1)S(1)} async-done(((bf16[4,2,512,128]{3,2,1,0:T(8,128)(2,1)}), bf16[4,2,512,128]{3,2,1,0:T(8,128)(2,1)S(1)}, u32[]{:S(2)}, u32[]{:S(2)}) %all-to-all-start.1) | async-done | bytes 1048608 | tf_op jit(solution)/shard_map/all_to_all | solution.py:217
  40.2 0.0 copy-start.1
  40.2 4.3 %shard_map.58 = (bf16[2,64,512]{2,1,0:T(8,128)(2,1)S(1)}, bf16[512,256]{1,0:T(8,128)(2,1)S(1)}) custom-call(bf16[2,512,2048]{2,1,0:T(8,128)(2,1)} %bitcast.13, bf16[2,2048,512]{2,1,0:T(8,128)(2,1)} %bitcast.12, bf16[4,2,512,128]{3,2,1,0:T(8,128)(2,1)S(1)} %all-to-all-done.1.first_ref, bf16[4,512,128]{2,1,0:T(8,128)(2,1)S(1)} %all-to-all-done.tile_ref.second_ref), custom_call_target="tpu_custom_call" | custom-call | flops 1610612736 | bytes 8388608 | tf_op jit(solution)/shard_map/pallas_call | solution.py:218
  44.5 0.0 collective-permute-done.1.refs_3_
  44.5 0.0 copy-done.1
  44.5 1.0 shard_map.59
  45.5 26.0 %all_to_all.25.in_ref = bf16[16,48,128]{2,1,0:T(8,128)(2,1)S(1)} all-to-all(bf16[16,48,128]{2,1,0:T(8,128)(2,1)S(1)} %shard_map.59), channel_id=1, replica_groups=mesh['sec'=3,'z'=4,'y'=8,'c'=2,'blk'=4] {'z','blk'}, dimensions={0} | all-to-all | bytes 393216 | tf_op jit(solution)/shard_map/all_to_all | solution.py:237
  71.6 16.1 %all_to_all.26.refs_1_ = bf16[8,4,32,128]{3,2,1,0:T(8,128)(2,1)S(1)} all-to-all(bf16[8,4,32,128]{3,2,1,0:T(8,128)(2,1)S(1)} %get-tuple-element.16), channel_id=1, replica_groups=mesh['sec'=3,'z'=4,'y'=8,'c'=2,'blk'=4] {'y'}, dimensions={0} | all-to-all | bytes 524288 | tf_op jit(solution)/shard_map/all_to_all | solution.py:241
  87.6 6.3 %collective-permute-start.2 = (bf16[8,4,32,128]{3,2,1,0:T(8,128)(2,1)S(1)}, bf16[8,4,32,128]{3,2,1,0:T(8,128)(2,1)S(1)}, u32[]{:S(2)}, u32[]{:S(2)}) collective-permute-start(bf16[8,4,32,128]{3,2,1,0:T(8,128)(2,1)S(1)} %all_to_all.26.refs_1_), channel_id=1, source_target_pairs={{0,4},{4,0},{1,5},{5,1},{2,6},{6,2},{3,7},{7,3},{8,12},{12,8},{9,1... | collective-permute-start | bytes 786440 | tf_op jit(solution)/shard_map/ppermute | solution.py:242
  93.9 1.1 %collective-permute-done.2.refs_2_ = bf16[8,4,32,128]{3,2,1,0:T(8,128)(2,1)S(1)} collective-permute-done((bf16[8,4,32,128]{3,2,1,0:T(8,128)(2,1)S(1)}, bf16[8,4,32,128]{3,2,1,0:T(8,128)(2,1)S(1)}, u32[]{:S(2)}, u32[]{:S(2)}) %collective-permute-start.2) | collective-permute-done | bytes 262176 | tf_op jit(solution)/shard_map/ppermute | solution.py:242
  95.1 2.6 %shard_map.61 = bf16[4,4,2,32,128]{4,3,2,1,0:T(8,128)(2,1)S(1)} custom-call(s32[4,8,128]{2,1,0:T(8,128)S(1)} %get-tuple-element.15.refs_0_, bf16[8,4,32,128]{3,2,1,0:T(8,128)(2,1)S(1)} %all_to_all.26.refs_1_, bf16[8,4,32,128]{3,2,1,0:T(8,128)(2,1)S(1)} %collective-permute-done.2.refs_2_), custom_call_target="tpu_custom_call" | custom-call | tf_op jit(solution)/shard_map/pallas_call | solution.py:243
  97.7 12.7 %all_to_all.27 = bf16[16,2,32,128]{3,2,1,0:T(8,128)(2,1)S(1)} all-to-all(bf16[16,2,32,128]{3,2,1,0:T(8,128)(2,1)S(1)} %bitcast.8), channel_id=1, replica_groups=mesh['sec'=3,'z'=4,'y'=8,'c'=2,'blk'=4] {'z','blk'}, dimensions={0} | all-to-all | bytes 524288 | tf_op jit(solution)/shard_map/all_to_all | solution.py:248
  110.4 0.7 convert_reduce_fusion
  (1 shorter events, 0.0 us)
Async XLA Ops:
  0.0 0.9 copy-start
  1.9 15.5 %all-to-all-start = ((bf16[4,512,128]{2,1,0:T(8,128)(2,1)}), bf16[4,512,128]{2,1,0:T(8,128)(2,1)S(1)}, u32[]{:S(2)}, u32[]{:S(2)}) async-start(bf16[4,512,128]{2,1,0:T(8,128)(2,1)} %get-tuple-element.12), calls=%async_computation | async-start | bytes 1048576 | tf_op jit(solution)/shard_map/all_to_all | solution.py:203
  6.7 16.9 %collective-permute-start = (bf16[512,128]{1,0:T(8,128)(2,1)S(1)}, bf16[512,128]{1,0:T(8,128)(2,1)S(1)}, u32[]{:S(2)}, u32[]{:S(2)}) collective-permute-start(bf16[512,128]{1,0:T(8,128)(2,1)S(1)} %get-tuple-element.11.own_ref), channel_id=1, source_target_pairs={{512,0},{0,256},{256,512},{513,1},{1,257},{257,513},{514,2},{2,258... | collective-permute-start | bytes 393224 | tf_op jit(solution)/shard_map/ppermute | solution.py:202
  24.7 15.4 %all-to-all-start.1 = ((bf16[4,2,512,128]{3,2,1,0:T(8,128)(2,1)}), bf16[4,2,512,128]{3,2,1,0:T(8,128)(2,1)S(1)}, u32[]{:S(2)}, u32[]{:S(2)}) async-start(bf16[4,2,512,128]{3,2,1,0:T(8,128)(2,1)} %shard_map.57), calls=%async_computation.1 | async-start | bytes 2097152 | tf_op jit(solution)/shard_map/all_to_all | solution.py:217
  29.6 14.9 %collective-permute-start.1 = (bf16[2,64,512]{2,1,0:T(8,128)(2,1)S(1)}, bf16[2,64,512]{2,1,0:T(8,128)(2,1)S(1)}, u32[]{:S(2)}, u32[]{:S(2)}) collective-permute-start(bf16[2,64,512]{2,1,0:T(8,128)(2,1)S(1)} %shard_map.56._), channel_id=1, source_target_pairs={{512,0},{0,256},{256,512},{513,1},{1,257},{257,513},{514,2},{2,258... | collective-permute-start | bytes 393224 | tf_op jit(solution)/shard_map/ppermute | solution.py:213
  40.2 4.3 %copy-start.1 = (s32[1,16,2]{1,2,0:T(2,128)S(1)}, s32[1,16,2]{1,2,0:T(2,128)}, u32[]{:S(2)}) copy-start(s32[1,16,2]{1,2,0:T(2,128)} %param.8) | copy-start | bytes 388
  87.6 7.4 %collective-permute-start.2 = (bf16[8,4,32,128]{3,2,1,0:T(8,128)(2,1)S(1)}, bf16[8,4,32,128]{3,2,1,0:T(8,128)(2,1)S(1)}, u32[]{:S(2)}, u32[]{:S(2)}) collective-permute-start(bf16[8,4,32,128]{3,2,1,0:T(8,128)(2,1)S(1)} %all_to_all.26.refs_1_), channel_id=1, source_target_pairs={{0,4},{4,0},{1,5},{5,1},{2,6},{6,2},{3,7},{7,3},{8,12},{12,8},{9,1... | collective-permute-start | bytes 786440 | tf_op jit(solution)/shard_map/ppermute | solution.py:242

commit v4 on v3

--- a/solution.py
+++ b/solution.py
@@ -12,7 +12,6 @@
 F32 = jnp.float32
 VMEM = pl.BlockSpec(memory_space=pltpu.VMEM)
 SMEM = pl.BlockSpec(memory_space=pltpu.SMEM)
-ANY = pl.BlockSpec(memory_space=pl.ANY)
 HBM = pl.BlockSpec(memory_space=pltpu.HBM)
 
 
@@ -20,28 +19,10 @@
     return lax.dot_general(a, b, (((ca,), (cb,)), ((), ())), preferred_element_type=F32)
 
 
-def swapped(x):
-    return pltpu.roll(x, x.shape[-1] // 2, x.ndim - 1)
-
-
-def lower(x):
-    return lax.broadcasted_iota(jnp.int32, x.shape, x.ndim - 1) < x.shape[-1] // 2
-
-
-def halves_kernel(tile_ref, first_ref, second_ref):
-    real = tile_ref[0].astype(F32)
-    imag = tile_ref[1].astype(F32)
-    first_ref[...] = jnp.where(lower(real), real, swapped(imag)).astype(BF16)
-    second = jnp.where(lower(real), swapped(real), imag).astype(BF16)
-    for j in range(second_ref.shape[0]):
-        second_ref[j] = second
-
-
-def copies_kernel(own_ref, other_ref, _, out_ref):
-    own, other = own_ref[...], other_ref[...]
+def spread_kernel(tile_ref, out_ref):
+    both = jnp.concatenate([tile_ref[0], tile_ref[1]], axis=1)
     for j in range(out_ref.shape[0]):
-        out_ref[j, 0] = own
-        out_ref[j, 1] = other
+        out_ref[j] = both
 
 
 def chunked(source, target, sems, dim, size):
@@ -53,62 +34,42 @@
     return copies
 
 
-def left_half(tile_of, beta_ref, copies):
-    acc_r = acc_i = None
-    for j, copy in enumerate(copies):
-        copy.wait()
-        tile = tile_of(j)
-        rows = tile.shape[0]
-        add_r = dot(tile, beta_ref[0, j * rows : (j + 1) * rows, :], 0, 0)
-        add_i = dot(tile, beta_ref[1, j * rows : (j + 1) * rows, :], 0, 0)
-        acc_r = add_r if acc_r is None else acc_r + add_r
-        acc_i = add_i if acc_i is None else acc_i + add_i
-    h = acc_r.shape[0] // 2
-    return acc_r[:h] + acc_i[h:], acc_i[:h] - acc_r[h:]
-
-
-def left_kernel(beta_hbm, tile_ref, left_ref, beta_ref, sems):
-    copies = chunked(beta_hbm, beta_ref, sems, 1, tile_ref.shape[1])
-    real, imag = left_half(lambda j: tile_ref[j], beta_ref, copies)
-    left_ref[0] = real.astype(BF16)
-    left_ref[1] = imag.astype(BF16)
-
-
-def middle_kernel(
-    tau_hbm, beta_hbm, first_ref, second_ref, left_ref, image_ref, beta_ref, tau_ref, sems
-):
-    parts, _, rows, k = first_ref.shape
-    beta_copies = chunked(beta_hbm, beta_ref, sems.at[0], 1, rows)
-    tau_copies = chunked(tau_hbm, tau_ref, sems.at[1], 2, rows)
-    real, imag = left_half(lambda j: first_ref[j, 1], beta_ref, beta_copies)
-    left_ref[0] = real.astype(BF16)
-    left_ref[1] = imag.astype(BF16)
-    acc_r = acc_i = None
+def product(on_real, on_imag):
+    k = on_real.shape[1] // 2
+    return jnp.concatenate(
+        [on_real[:, :k] - on_imag[:, k:], on_real[:, k:] + on_imag[:, :k]], axis=1
+    )
+
+
+def legs_kernel(tau_hbm, beta_hbm, tile_ref, out_ref, tau_ref, beta_ref, sems):
+    parts, rows, _ = tile_ref.shape
+    tau_copies = chunked(tau_hbm, tau_ref, sems.at[0], 2, rows)
+    beta_copies = chunked(beta_hbm, beta_ref, sems.at[1], 1, rows)
+    on_real = on_imag = None
     for j in range(parts):
         tau_copies[j].wait()
-        both = jnp.concatenate([first_ref[j, 0], second_ref[j]], axis=1)
-        add_r = dot(tau_ref[0, :, j * rows : (j + 1) * rows], both, 1, 0)
-        add_i = dot(tau_ref[1, :, j * rows : (j + 1) * rows], both, 1, 0)
-        acc_r = add_r if acc_r is None else acc_r + add_r
-        acc_i = add_i if acc_i is None else acc_i + add_i
-    for h in range(2):
-        a, b = acc_r[:, h * k : (h + 1) * k], swapped(acc_i[:, h * k : (h + 1) * k])
-        image_ref[:, h * k : (h + 1) * k] = (a + jnp.where(lower(b), -b, b)).astype(BF16)
-
-
-def pack_kernel(scale, lists_ref, load_ref, first_ref, second_ref, image_ref, out_ref):
+        add_real = dot(tau_ref[0, :, j * rows : (j + 1) * rows], tile_ref[j], 1, 0)
+        add_imag = dot(tau_ref[1, :, j * rows : (j + 1) * rows], tile_ref[j], 1, 0)
+        on_real = add_real if on_real is None else on_real + add_real
+        on_imag = add_imag if on_imag is None else on_imag + add_imag
+    image = product(on_real, on_imag).astype(BF16)
+    for j in range(parts):
+        beta_copies[j].wait()
+        out_ref[j] = product(
+            dot(beta_ref[0, j * rows : (j + 1) * rows, :], image, 1, 0),
+            dot(beta_ref[1, j * rows : (j + 1) * rows, :], image, 1, 0),
+        ).astype(BF16)
+
+
+def pack_kernel(scale, lists_ref, load_ref, parts_ref, sink_ref, out_ref):
     slices = out_ref.shape[0]
-    k = image_ref.shape[1] // 2
-    image = image_ref[...]
-    from_r = dot(jnp.concatenate([first_ref[0], second_ref[0]], axis=0), image, 1, 0)
-    from_i = dot(jnp.concatenate([first_ref[1], second_ref[1]], axis=0), image, 1, 0)
-    halves = []
-    for h in range(2):
-        a, b = from_r[:, h * k : (h + 1) * k], swapped(from_i[:, h * k : (h + 1) * k])
-        halves.append(a + jnp.where(lower(b), -b, b))
-    first, second = halves
-    real = jnp.where(lower(first), first, swapped(second)) * scale
-    imag = jnp.where(lower(first), swapped(first), second) * scale
+    k = sink_ref.shape[2]
+    dressed = parts_ref[0].astype(F32)
+    for j in range(1, parts_ref.shape[0]):
+        dressed = dressed + parts_ref[j].astype(F32)
+    dressed = dressed.astype(BF16)
+    both = product(dot(sink_ref[0], dressed, 0, 0), -dot(sink_ref[1], dressed, 0, 0)) * scale
+    real, imag = both[:, :k], both[:, k:]
     cut = [x.reshape(slices, k // slices, k) for x in (real.T, imag.T, real, imag)]
     packed = jnp.concatenate(cut, axis=1).astype(BF16)
     n = packed.shape[1]
@@ -195,45 +156,28 @@
     slices = nz * nx
     w = k // slices
     quarter = k // nx
-    onward = [((i - 1) % ns, i) for i in range(ns)]
-    work = 4 * k * order * share
-
-    first, second = call(halves_kernel, [((share, k), BF16), ((nx, share, k), BF16)], [VMEM])(tile)
-    first_before = lax.ppermute(first, "sec", onward)
-    seconds = lax.all_to_all(second, "blk", 0, 0, tiled=True)
-    (left_second,) = call(
-        left_kernel,
-        [((2, k // 2, share), BF16)],
-        [HBM, VMEM],
-        [pltpu.VMEM(beta.shape, BF16), pltpu.SemaphoreType.DMA((nx,))],
-        work,
-        2**22,
-        16,
-    )(beta, seconds)
-    left_before = lax.ppermute(left_second, "sec", onward)
-    (copies,) = call(copies_kernel, [((nx, 2, share, k), BF16)], [VMEM, VMEM, ANY])(
-        first, first_before, left_second
-    )
-    firsts = lax.all_to_all(copies, "blk", 0, 0, tiled=True)
-    left_first, image = call(
-        middle_kernel,
-        [((2, k // 2, share), BF16), ((share, 2 * k), BF16)],
-        [HBM, HBM, VMEM, VMEM],
+
+    before = lax.ppermute(tile, "sec", [((i - 1) % ns, i) for i in range(ns)])
+    (tiles,) = call(spread_kernel, [((nx, share, 2 * k), BF16)], [VMEM])(tile)
+    tiles = lax.all_to_all(tiles, "blk", 0, 0, tiled=True)
+    (dressed,) = call(
+        legs_kernel,
+        [((nx, share, 2 * k), BF16)],
+        [HBM, HBM, VMEM],
         [
+            pltpu.VMEM(tau.shape, BF16),
             pltpu.VMEM(beta.shape, BF16),
-            pltpu.VMEM(tau.shape, BF16),
             pltpu.SemaphoreType.DMA((2, nx)),
         ],
-        3 * work,
+        16 * k * order * share,
         2**23,
-        16,
-    )(tau, beta, firsts, seconds)
-
+    )(tau, beta, tiles)
+    dressed = lax.all_to_all(dressed, "blk", 0, 0, tiled=True)
     (packed,) = call(
         lambda *refs: pack_kernel(order**-0.5, *refs),
         [((slices, 4 * w + 16, k), BF16)],
-        [SMEM, SMEM, VMEM, VMEM, VMEM],
-    )(diagrams[0].T, owner_loads, left_first, left_before, image)
+        [SMEM, SMEM, VMEM, VMEM],
+    )(diagrams[0].T, owner_loads, dressed, before)
     packed = lax.all_to_all(packed, ("z", "blk"), 0, 0, tiled=True)
     pieces, numbers = call(
         sum_kernel, [((ny, nz, 4 * w, k), BF16), ((nz, 8, k), jnp.int32)], [VMEM]

time: 111 us -> 124 us (1.12)
  blocking collectives: 54.7 us -> 78.4 us
  starting transfers between devices: 30.5 us -> 23.9 us
  Pallas kernels: 12.6 us -> 9.43 us
  waiting for transfers between devices: 10.9 us -> 9.17 us
    all_to_all x0 -> x1, blocking collectives: none -> 14.4 us  [on_device(): tiles = lax.all_to_all(tiles, 'blk', 0, 0, tiled=True)]
    all_to_all x1, blocking collectives: 26 us -> 34.1 us  [on_device(): packed = lax.all_to_all(packed, ('z', 'blk'), 0, 0, tiled=True)]
    all_to_all x2 -> x1, waiting for transfers between devices: 6 us -> 0.01 us  [on_device(): dressed = lax.all_to_all(dressed, 'blk', 0, 0, tiled=True)]
    all_to_all x2 -> x1, starting transfers between devices: 9.07 us -> 3.53 us  [on_device(): dressed = lax.all_to_all(dressed, 'blk', 0, 0, tiled=True)]
    ppermute x2 -> x1, waiting for transfers between devices: 3.72 us -> 8.02 us  [on_device(): before = lax.ppermute(tile, 'sec', [((i - 1) % ns, i) for i in range(ns)])]
    pallas_call x4 -> x2, Pallas kernels: 8.9 us -> 5.82 us  [the longest x1 5.75 us: on_device(): call(legs_kernel, [((nx, share, 2 * k), BF16)], [HBM, HBM, VMEM], [pltpu....]
    ppermute x2 -> x1, starting transfers between devices: 15.2 us -> 15.1 us  [on_device(): before = lax.ppermute(tile, 'sec', [((i - 1) % ns, i) for i in range(ns)])]
  transfers between devices with their start and end apart: 5 -> 3, of which waited for: 3 -> 2; matrix products, arithmetic and copies ran while one was open for 0% -> 0% of each run, Pallas kernels for 6% -> 0%
where the time goes in v4:
time: 124 us; the launch traced here: 123 us
  blocking collectives  78.4 us (63%)
  starting transfers between devices  23.9 us (19%)
  Pallas kernels  9.43 us (8%)
  waiting for transfers between devices  9.17 us (7%)
    all_to_all x1, blocking collectives, on_device(): packed = lax.all_to_all(packed, ('z', 'blk'), 0, 0, tiled=True)  34.1 us
    all_to_all x1, blocking collectives, on_device(): pieces = lax.all_to_all(pieces, 'y', 0, 0, tiled=True)  16.1 us
    ppermute x1, starting transfers between devices, on_device(): before = lax.ppermute(tile, 'sec', [((i - 1) % ns, i) for i in range(ns)])  15.1 us
    all_to_all x1, blocking collectives, on_device(): tiles = lax.all_to_all(tiles, 'blk', 0, 0, tiled=True)  14.4 us
    all_to_all x1, blocking collectives, on_device(): lax.all_to_all(partial.reshape(slices, 2, quarter, k), ('z', 'blk'), 0, 0...  13.9 us
    ppermute x1, waiting for transfers between devices, on_device(): before = lax.ppermute(tile, 'sec', [((i - 1) % ns, i) for i in range(ns)])  8.02 us
    pallas_call x1, Pallas kernels, on_device(): call(legs_kernel, [((nx, share, 2 * k), BF16)], [HBM, HBM, VMEM], [pltpu....  5.75 us
    ppermute x1, starting transfers between devices, on_device(): others = lax.ppermute(pieces, 'c', [(i, (i + 1) % nc) for i in range(nc)])  5.27 us
  transfers between devices with their start and end apart: 3, of which 2 were waited for; matrix products, arithmetic and copies ran while one was open for 0% of the time, Pallas kernels for 0%

profile of v4, /device:TPU:1, one launch (start us, length us, event | category | flops | bytes accessed | tf_op | source)
XLA Modules:
  0.0 123.2 jit_solution(11667796933771446733)
XLA Ops:
  0.0 0.0 copy-start
  0.0 0.9 copy-done
  1.0 0.1 shard_map.55
  1.0 14.4 %all_to_all.25.tile_ref = bf16[4,512,256]{2,1,0:T(8,128)(2,1)S(1)} all-to-all(bf16[4,512,256]{2,1,0:T(8,128)(2,1)S(1)} %shard_map.55), channel_id=1, replica_groups=mesh['sec'=3,'z'=4,'y'=8,'c'=2,'blk'=4] {'blk'}, dimensions={0} | all-to-all | bytes 2097152 | tf_op jit(solution)/shard_map/all_to_all | solution.py:162
  15.4 0.0 copy-start.1
  15.4 0.0 copy-start.2
  15.4 5.8 %shard_map.56 = bf16[4,512,256]{2,1,0:T(8,128)(2,1)} custom-call(bf16[2,512,2048]{2,1,0:T(8,128)(2,1)} %bitcast.12, bf16[2,2048,512]{2,1,0:T(8,128)(2,1)} %bitcast.13, bf16[4,512,256]{2,1,0:T(8,128)(2,1)S(1)} %all_to_all.25.tile_ref), custom_call_target="tpu_custom_call" | custom-call | flops 2147483648 | bytes 8388608 | tf_op jit(solution)/shard_map/pallas_call | solution.py:163
  21.2 3.5 %all-to-all-start.1 = ((bf16[4,512,256]{2,1,0:T(8,128)(2,1)}), bf16[4,512,256]{2,1,0:T(8,128)(2,1)S(1)}, u32[]{:S(2)}, u32[]{:S(2)}) async-start(bf16[4,512,256]{2,1,0:T(8,128)(2,1)} %shard_map.56), calls=%async_computation.1 | async-start | bytes 2097152 | tf_op jit(solution)/shard_map/all_to_all | solution.py:175
  24.7 0.0 copy-done.1
  24.7 15.1 %collective-permute-start = (bf16[2,512,128]{2,1,0:T(8,128)(2,1)S(1)}, bf16[2,512,128]{2,1,0:T(8,128)(2,1)S(1)}, u32[]{:S(2)}, u32[]{:S(2)}) collective-permute-start(bf16[2,512,128]{2,1,0:T(8,128)(2,1)S(1)} %bitcast.10), channel_id=1, source_target_pairs={{512,0},{0,256},{256,512},{513,1},{1,257},{257,513},{514,2},{2,258... | collective-permute-start | bytes 786440 | tf_op jit(solution)/shard_map/ppermute | solution.py:160
  40.5 8.0 %collective-permute-done.refs_3_ = bf16[2,512,128]{2,1,0:T(8,128)(2,1)S(1)} collective-permute-done((bf16[2,512,128]{2,1,0:T(8,128)(2,1)S(1)}, bf16[2,512,128]{2,1,0:T(8,128)(2,1)S(1)}, u32[]{:S(2)}, u32[]{:S(2)}) %collective-permute-start) | collective-permute-done | bytes 262176 | tf_op jit(solution)/shard_map/ppermute | solution.py:160
  48.5 0.0 all-to-all-done.1.refs_2_
  48.5 0.0 copy-done.2
  48.5 0.9 shard_map.57
  49.5 34.1 %all_to_all.26.in_ref = bf16[16,48,128]{2,1,0:T(8,128)(2,1)S(1)} all-to-all(bf16[16,48,128]{2,1,0:T(8,128)(2,1)S(1)} %shard_map.57), channel_id=1, replica_groups=mesh['sec'=3,'z'=4,'y'=8,'c'=2,'blk'=4] {'z','blk'}, dimensions={0} | all-to-all | bytes 393216 | tf_op jit(solution)/shard_map/all_to_all | solution.py:181
  83.6 16.1 %all_to_all.27.refs_1_ = bf16[8,4,32,128]{3,2,1,0:T(8,128)(2,1)S(1)} all-to-all(bf16[8,4,32,128]{3,2,1,0:T(8,128)(2,1)S(1)} %get-tuple-element.8), channel_id=1, replica_groups=mesh['sec'=3,'z'=4,'y'=8,'c'=2,'blk'=4] {'y'}, dimensions={0} | all-to-all | bytes 524288 | tf_op jit(solution)/shard_map/all_to_all | solution.py:185
  99.6 5.3 %collective-permute-start.1 = (bf16[8,4,32,128]{3,2,1,0:T(8,128)(2,1)S(1)}, bf16[8,4,32,128]{3,2,1,0:T(8,128)(2,1)S(1)}, u32[]{:S(2)}, u32[]{:S(2)}) collective-permute-start(bf16[8,4,32,128]{3,2,1,0:T(8,128)(2,1)S(1)} %all_to_all.27.refs_1_), channel_id=1, source_target_pairs={{0,4},{4,0},{1,5},{5,1},{2,6},{6,2},{3,7},{7,3},{8,12},{12,8},{9,1... | collective-permute-start | bytes 786440 | tf_op jit(solution)/shard_map/ppermute | solution.py:186
  104.9 1.1 collective-permute-done.1.refs_2_
  106.0 2.6 %shard_map.59 = bf16[4,4,2,32,128]{4,3,2,1,0:T(8,128)(2,1)S(1)} custom-call(s32[4,8,128]{2,1,0:T(8,128)S(1)} %get-tuple-element.7.refs_0_, bf16[8,4,32,128]{3,2,1,0:T(8,128)(2,1)S(1)} %all_to_all.27.refs_1_, bf16[8,4,32,128]{3,2,1,0:T(8,128)(2,1)S(1)} %collective-permute-done.1.refs_2_), custom_call_target="tpu_custom_call" | custom-call | tf_op jit(solution)/shard_map/pallas_call | solution.py:187
  108.7 13.9 %all_to_all.28 = bf16[16,2,32,128]{3,2,1,0:T(8,128)(2,1)S(1)} all-to-all(bf16[16,2,32,128]{3,2,1,0:T(8,128)(2,1)S(1)} %bitcast.8), channel_id=1, replica_groups=mesh['sec'=3,'z'=4,'y'=8,'c'=2,'blk'=4] {'z','blk'}, dimensions={0} | all-to-all | bytes 524288 | tf_op jit(solution)/shard_map/all_to_all | solution.py:192
  122.6 0.7 convert_reduce_fusion
  (1 shorter events, 0.0 us)
Async XLA Ops:
  0.0 0.9 copy-start
  15.4 9.3 %copy-start.1 = (bf16[1,1,2,512,128]{4,3,2,1,0:T(8,128)(2,1)S(1)}, bf16[1,1,2,512,128]{4,3,2,1,0:T(8,128)(2,1)}, u32[]{:S(2)}) copy-start(bf16[1,1,2,512,128]{4,3,2,1,0:T(8,128)(2,1)} %param.7) | copy-start | bytes 786436
  15.4 33.1 %copy-start.2 = (s32[1,16,2]{1,2,0:T(2,128)S(1)}, s32[1,16,2]{1,2,0:T(2,128)}, u32[]{:S(2)}) copy-start(s32[1,16,2]{1,2,0:T(2,128)} %param.8) | copy-start | bytes 388
  21.2 27.4 %all-to-all-start.1 = ((bf16[4,512,256]{2,1,0:T(8,128)(2,1)}), bf16[4,512,256]{2,1,0:T(8,128)(2,1)S(1)}, u32[]{:S(2)}, u32[]{:S(2)}) async-start(bf16[4,512,256]{2,1,0:T(8,128)(2,1)} %shard_map.56), calls=%async_computation.1 | async-start | bytes 2097152 | tf_op jit(solution)/shard_map/all_to_all | solution.py:175
  24.7 23.8 %collective-permute-start = (bf16[2,512,128]{2,1,0:T(8,128)(2,1)S(1)}, bf16[2,512,128]{2,1,0:T(8,128)(2,1)S(1)}, u32[]{:S(2)}, u32[]{:S(2)}) collective-permute-start(bf16[2,512,128]{2,1,0:T(8,128)(2,1)S(1)} %bitcast.10), channel_id=1, source_target_pairs={{512,0},{0,256},{256,512},{513,1},{1,257},{257,513},{514,2},{2,258... | collective-permute-start | bytes 786440 | tf_op jit(solution)/shard_map/ppermute | solution.py:160
  99.6 6.4 %collective-permute-start.1 = (bf16[8,4,32,128]{3,2,1,0:T(8,128)(2,1)S(1)}, bf16[8,4,32,128]{3,2,1,0:T(8,128)(2,1)S(1)}, u32[]{:S(2)}, u32[]{:S(2)}) collective-permute-start(bf16[8,4,32,128]{3,2,1,0:T(8,128)(2,1)S(1)} %all_to_all.27.refs_1_), channel_id=1, source_target_pairs={{0,4},{4,0},{1,5},{5,1},{2,6},{6,2},{3,7},{7,3},{8,12},{12,8},{9,1... | collective-permute-start | bytes 786440 | tf_op jit(solution)/shard_map/ppermute | solution.py:186
